TPU v7x, 256 devices: a whole 4x4x8 slice. The times are simulated.
256 devices in a mesh: dp: 16 (over y_hi, z), blk: 16 (over x, y_lo, core).
Axes of the slice: x: 4, y: 4 (y_hi: 2, y_lo: 2; y = y_hi * 2 + y_lo), z: 8, core: 2. Of those that a mesh axis runs over, the one named last changes fastest.
Arguments:
- visual_summary_vectors: bfloat16 [32768, 1792], P(('dp', 'blk')), may hold values from -24 to 24
- caption_summary_vectors: bfloat16 [32768, 1280], P(('dp', 'blk')), may hold values from -24 to 24
- pairing_identifiers: int32 [32768], P('dp'), may hold values from 0 to 1023
- valid_sample_tally: int32 [16, 16], P('dp'), may hold values from 64 to 128, as said below
- visual_mapping_matrix: bfloat16 [1792, 1536], replicated, may hold values from -0.125 to 0.125
- caption_mapping_matrix: bfloat16 [1280, 1536], replicated, may hold values from -0.15625 to 0.15625
- sharpness_factor: float32 [1], replicated, may hold values from 4 to 16
- score_shift_term: float32 [1], replicated, may hold values from -3 to -1
Outputs:
- per_sample_cost: float32 [32768], P(('dp', 'blk'))
- grad_image: float32 [1792, 1536], P('blk')
- grad_text: float32 [1280, 1536], P('blk')
Inputs may be any that keep to these rules, and one draw needn't show every extreme that they name: `pairing_identifiers`: rows of one group with equal labels are positive pairs; a row's image and text share its label. `valid_sample_tally`: some device is full in every draw.
All inputs are finite; a program needn't handle non-finite values.
Results may differ from a plain program's by a relative error of at most 0.011.
Values may be sent and summed in bfloat16 or wider, within the bound.
A program may use at most 128 MiB of HBM per device.

v0:
```python
import jax
import jax.numpy as jnp
from jax import lax
from jax.sharding import PartitionSpec as P

loss_scale = 256.0
epsilon = 1e-06


def shifted(block, axis, distance):
    devices = range(lax.axis_size(axis))
    route = [((i - distance) % len(devices), i) for i in devices]
    return lax.ppermute(block, axis, route)


def project(source, weights):
    projected = jnp.dot(source, weights, preferred_element_type=jnp.float32)
    length = jnp.sqrt(jnp.sum(projected * projected, axis=1, keepdims=True) + epsilon)
    return (projected / length, length)


def unit_backward(unit_rows, length, grad_unit):
    radial = jnp.sum(unit_rows * grad_unit, axis=1, keepdims=True)
    return ((grad_unit - unit_rows * radial) / length).astype(jnp.bfloat16)


def reduce_over_samples(left, right):
    return lax.dot_general(
        left, right, (((0,), (0,)), ((), ())), preferred_element_type=jnp.float32
    )


def on_device(
    visual_summary_vectors,
    caption_summary_vectors,
    pairing_identifiers,
    valid_sample_tally,
    visual_mapping_matrix,
    caption_mapping_matrix,
    sharpness_factor,
    score_shift_term,
):
    local_rows = visual_summary_vectors.shape[0]
    block_count = lax.axis_size("blk")
    my_index = lax.axis_index("blk")
    embed_width = visual_mapping_matrix.shape[1]
    score_sharpness = sharpness_factor[0]
    additive_shift = score_shift_term[0]
    pair_scale = loss_scale / (block_count * local_rows)
    unit_img, len_img = project(visual_summary_vectors, visual_mapping_matrix)
    unit_txt, len_txt = project(caption_summary_vectors, caption_mapping_matrix)
    visual_normalized_vector = unit_img.astype(jnp.bfloat16)
    caption_normalized_vector = unit_txt.astype(jnp.bfloat16)
    group_counts = valid_sample_tally[0]
    block_ids = jnp.arange(block_count)
    my_limit = jnp.sum(jnp.where(block_ids == my_index, group_counts, 0))
    alive_image = jnp.arange(local_rows) < my_limit
    my_labels = lax.dynamic_slice_in_dim(pairing_identifiers, my_index * local_rows, local_rows)

    def pair_terms(text_piece, first_row):
        piece_rows = text_piece.shape[0]
        positions = first_row + jnp.arange(piece_rows)
        owners = positions // local_rows
        range_bounds = jnp.sum(
            jnp.where(owners[:, None] == block_ids[None, :], group_counts[None, :], 0), axis=1
        )
        alive_text = positions - owners * local_rows < range_bounds
        piece_labels = lax.dynamic_slice_in_dim(pairing_identifiers, first_row, piece_rows)
        angular_similarity = lax.dot_general(
            visual_normalized_vector,
            text_piece,
            (((1,), (1,)), ((), ())),
            preferred_element_type=jnp.float32,
        )
        similarity_scores = score_sharpness * angular_similarity + additive_shift
        target_sign = jnp.where(my_labels[:, None] == piece_labels[None, :], 1.0, -1.0)
        weight = jnp.where(alive_image[:, None] & alive_text[None, :], 1.0, 0.0)
        row_part = jnp.sum(jax.nn.softplus(-target_sign * similarity_scores) * weight, axis=1)
        sigmoid_derivatives = (
            -target_sign * jax.nn.sigmoid(-target_sign * similarity_scores) * weight * pair_scale
        ).astype(jnp.bfloat16)
        derivative_piece = score_sharpness * jnp.dot(
            sigmoid_derivatives, text_piece, preferred_element_type=jnp.float32
        )
        interim_quantity = (
            score_sharpness * reduce_over_samples(sigmoid_derivatives, visual_normalized_vector)
        ).astype(jnp.bfloat16)
        return (row_part, derivative_piece, interim_quantity)

    def rotation_step(turn_index, carried):
        travel_text, travel_grad, loss_sum, grad_sum = carried
        source_block = (my_index - turn_index) % block_count
        row_part, derivative_piece, interim_quantity = pair_terms(
            travel_text, source_block * local_rows
        )
        travel_grad = travel_grad + lax.optimization_barrier(interim_quantity).astype(jnp.float32)
        travel_text = shifted(travel_text, "blk", 1)
        travel_grad = shifted(travel_grad, "blk", 1)
        return (travel_text, travel_grad, loss_sum + row_part, grad_sum + derivative_piece)

    start_state = (
        caption_normalized_vector,
        jnp.zeros((local_rows, embed_width), jnp.float32),
        jnp.zeros((local_rows,), jnp.float32),
        jnp.zeros((local_rows, embed_width), jnp.float32),
    )
    _, grad_ztxt, loss_sum, derivative_visual_unit = lax.fori_loop(
        0, block_count, rotation_step, start_state
    )
    visual_change = unit_backward(unit_img, len_img, derivative_visual_unit)
    caption_change = unit_backward(unit_txt, len_txt, grad_ztxt)
    grad_image = lax.psum_scatter(
        reduce_over_samples(visual_summary_vectors, visual_change),
        "blk",
        scatter_dimension=0,
        tiled=True,
    )
    grad_text = lax.psum_scatter(
        reduce_over_samples(caption_summary_vectors, caption_change),
        "blk",
        scatter_dimension=0,
        tiled=True,
    )
    grad_image, grad_text = lax.psum((grad_image, grad_text), "dp")
    return (loss_sum / (block_count * local_rows), grad_image, grad_text)


def solution(mesh):
    placed = (
        P(("dp", "blk"), None),
        P(("dp", "blk"), None),
        P("dp"),
        P("dp", None),
        P(),
        P(),
        P(),
        P(),
    )
    return jax.shard_map(
        on_device,
        mesh=mesh,
        in_specs=placed,
        out_specs=(P(("dp", "blk")), P("blk", None), P("blk", None)),
        check_vma=False,
    )
```

profile of v0, /device:TPU:1, one launch (start us, length us, event | category | flops | bytes accessed | tf_op | source)
XLA Modules:
  0.0 822.2 jit_solution(6473590541133334530)
XLA Ops:
  8.8 3.5 multiply_reduce_fusion.2
  15.1 388.7 %while.22 = (s32[]{:T(128)}, bf16[128,1536]{1,0:T(8,128)(2,1)}, f32[128,1536]{1,0:T(8,128)S(1)}, f32[128]{0:T(128)S(1)}, f32[128,1536]{1,0:T(8,128)S(1)}, /*inde...) while((s32[]{:T(128)}, bf16[128,1536]{1,0:T(8,128)(2,1)}, ...), condition=%wide.region_6.7_spmd.clone, body=%wide.region_3.6_spmd.clone.sunk | while | flops 153037328 | bytes 11216399 | solution.py:107
  17.6 2.6 fusion.47
  20.2 2.0 fusion.48
  22.3 2.8 collective-permute-start.1
  26.2 12.0 %collective-permute-done = bf16[128,1536]{1,0:T(8,128)(2,1)} collective-permute-done((bf16[128,1536]{1,0:T(8,128)(2,1)S(1)}, bf16[128,1536]{1,0:T(8,128)(2,1)}, u32[]{:S(2)}, u32[]{:S(2)}) %collective-permute-start) | collective-permute-done | bytes 393248 | tf_op jit(solution)/shard_map/while/body/eval_jaxpr/ppermute | solution.py:13
  40.7 2.6 fusion.47
  43.3 2.0 fusion.48
  45.3 2.7 collective-permute-start.1
  49.2 12.0 %collective-permute-done = bf16[128,1536]{1,0:T(8,128)(2,1)} collective-permute-done((bf16[128,1536]{1,0:T(8,128)(2,1)S(1)}, bf16[128,1536]{1,0:T(8,128)(2,1)}, u32[]{:S(2)}, u32[]{:S(2)}) %collective-permute-start) | collective-permute-done | bytes 393248 | tf_op jit(solution)/shard_map/while/body/eval_jaxpr/ppermute | solution.py:13
  63.6 2.6 fusion.47
  66.2 2.0 fusion.48
  68.3 2.7 collective-permute-start.1
  72.1 12.0 %collective-permute-done = bf16[128,1536]{1,0:T(8,128)(2,1)} collective-permute-done((bf16[128,1536]{1,0:T(8,128)(2,1)S(1)}, bf16[128,1536]{1,0:T(8,128)(2,1)}, u32[]{:S(2)}, u32[]{:S(2)}) %collective-permute-start) | collective-permute-done | bytes 393248 | tf_op jit(solution)/shard_map/while/body/eval_jaxpr/ppermute | solution.py:13
  86.6 2.6 fusion.47
  89.2 2.0 fusion.48
  91.2 2.7 collective-permute-start.1
  95.7 11.4 %collective-permute-done = bf16[128,1536]{1,0:T(8,128)(2,1)} collective-permute-done((bf16[128,1536]{1,0:T(8,128)(2,1)S(1)}, bf16[128,1536]{1,0:T(8,128)(2,1)}, u32[]{:S(2)}, u32[]{:S(2)}) %collective-permute-start) | collective-permute-done | bytes 393248 | tf_op jit(solution)/shard_map/while/body/eval_jaxpr/ppermute | solution.py:13
  109.5 2.6 fusion.47
  112.1 2.0 fusion.48
  114.2 2.7 collective-permute-start.1
  119.5 10.5 %collective-permute-done = bf16[128,1536]{1,0:T(8,128)(2,1)} collective-permute-done((bf16[128,1536]{1,0:T(8,128)(2,1)S(1)}, bf16[128,1536]{1,0:T(8,128)(2,1)}, u32[]{:S(2)}, u32[]{:S(2)}) %collective-permute-start) | collective-permute-done | bytes 393248 | tf_op jit(solution)/shard_map/while/body/eval_jaxpr/ppermute | solution.py:13
  132.5 2.6 fusion.47
  135.1 2.0 fusion.48
  137.1 2.7 collective-permute-start.1
  139.8 2.5 collective-permute-start
  143.4 9.9 %collective-permute-done = bf16[128,1536]{1,0:T(8,128)(2,1)} collective-permute-done((bf16[128,1536]{1,0:T(8,128)(2,1)S(1)}, bf16[128,1536]{1,0:T(8,128)(2,1)}, u32[]{:S(2)}, u32[]{:S(2)}) %collective-permute-start) | collective-permute-done | bytes 393248 | tf_op jit(solution)/shard_map/while/body/eval_jaxpr/ppermute | solution.py:13
  155.8 2.6 fusion.47
  158.4 1.9 fusion.48
  160.4 2.3 collective-permute-start.1
  162.7 3.4 collective-permute-start
  167.2 11.1 %collective-permute-done = bf16[128,1536]{1,0:T(8,128)(2,1)} collective-permute-done((bf16[128,1536]{1,0:T(8,128)(2,1)S(1)}, bf16[128,1536]{1,0:T(8,128)(2,1)}, u32[]{:S(2)}, u32[]{:S(2)}) %collective-permute-start) | collective-permute-done | bytes 393248 | tf_op jit(solution)/shard_map/while/body/eval_jaxpr/ppermute | solution.py:13
  180.8 2.6 fusion.47
  185.7 4.3 collective-permute-start
  191.1 12.3 %collective-permute-done = bf16[128,1536]{1,0:T(8,128)(2,1)} collective-permute-done((bf16[128,1536]{1,0:T(8,128)(2,1)S(1)}, bf16[128,1536]{1,0:T(8,128)(2,1)}, u32[]{:S(2)}, u32[]{:S(2)}) %collective-permute-start) | collective-permute-done | bytes 393248 | tf_op jit(solution)/shard_map/while/body/eval_jaxpr/ppermute | solution.py:13
  205.9 2.6 fusion.47
  210.6 3.2 collective-permute-start
  214.9 13.5 %collective-permute-done = bf16[128,1536]{1,0:T(8,128)(2,1)} collective-permute-done((bf16[128,1536]{1,0:T(8,128)(2,1)S(1)}, bf16[128,1536]{1,0:T(8,128)(2,1)}, u32[]{:S(2)}, u32[]{:S(2)}) %collective-permute-start) | collective-permute-done | bytes 393248 | tf_op jit(solution)/shard_map/while/body/eval_jaxpr/ppermute | solution.py:13
  230.9 2.6 fusion.47
  235.7 2.0 collective-permute-start
  238.8 14.7 %collective-permute-done = bf16[128,1536]{1,0:T(8,128)(2,1)} collective-permute-done((bf16[128,1536]{1,0:T(8,128)(2,1)S(1)}, bf16[128,1536]{1,0:T(8,128)(2,1)}, u32[]{:S(2)}, u32[]{:S(2)}) %collective-permute-start) | collective-permute-done | bytes 393248 | tf_op jit(solution)/shard_map/while/body/eval_jaxpr/ppermute | solution.py:13
  256.0 2.6 fusion.47
  262.6 16.0 %collective-permute-done = bf16[128,1536]{1,0:T(8,128)(2,1)} collective-permute-done((bf16[128,1536]{1,0:T(8,128)(2,1)S(1)}, bf16[128,1536]{1,0:T(8,128)(2,1)}, u32[]{:S(2)}, u32[]{:S(2)}) %collective-permute-start) | collective-permute-done | bytes 393248 | tf_op jit(solution)/shard_map/while/body/eval_jaxpr/ppermute | solution.py:13
  281.1 2.6 fusion.47
  287.0 16.6 %collective-permute-done = bf16[128,1536]{1,0:T(8,128)(2,1)} collective-permute-done((bf16[128,1536]{1,0:T(8,128)(2,1)S(1)}, bf16[128,1536]{1,0:T(8,128)(2,1)}, u32[]{:S(2)}, u32[]{:S(2)}) %collective-permute-start) | collective-permute-done | bytes 393248 | tf_op jit(solution)/shard_map/while/body/eval_jaxpr/ppermute | solution.py:13
  306.1 2.6 fusion.47
  312.0 16.6 %collective-permute-done = bf16[128,1536]{1,0:T(8,128)(2,1)} collective-permute-done((bf16[128,1536]{1,0:T(8,128)(2,1)S(1)}, bf16[128,1536]{1,0:T(8,128)(2,1)}, u32[]{:S(2)}, u32[]{:S(2)}) %collective-permute-start) | collective-permute-done | bytes 393248 | tf_op jit(solution)/shard_map/while/body/eval_jaxpr/ppermute | solution.py:13
  331.2 2.6 fusion.47
  337.1 16.6 %collective-permute-done = bf16[128,1536]{1,0:T(8,128)(2,1)} collective-permute-done((bf16[128,1536]{1,0:T(8,128)(2,1)S(1)}, bf16[128,1536]{1,0:T(8,128)(2,1)}, u32[]{:S(2)}, u32[]{:S(2)}) %collective-permute-start) | collective-permute-done | bytes 393248 | tf_op jit(solution)/shard_map/while/body/eval_jaxpr/ppermute | solution.py:13
  356.2 2.6 fusion.47
  362.1 16.6 %collective-permute-done = bf16[128,1536]{1,0:T(8,128)(2,1)} collective-permute-done((bf16[128,1536]{1,0:T(8,128)(2,1)S(1)}, bf16[128,1536]{1,0:T(8,128)(2,1)}, u32[]{:S(2)}, u32[]{:S(2)}) %collective-permute-start) | collective-permute-done | bytes 393248 | tf_op jit(solution)/shard_map/while/body/eval_jaxpr/ppermute | solution.py:13
  381.3 2.6 fusion.47
  387.2 16.6 %collective-permute-done = bf16[128,1536]{1,0:T(8,128)(2,1)} collective-permute-done((bf16[128,1536]{1,0:T(8,128)(2,1)S(1)}, bf16[128,1536]{1,0:T(8,128)(2,1)}, u32[]{:S(2)}, u32[]{:S(2)}) %collective-permute-start) | collective-permute-done | bytes 393248 | tf_op jit(solution)/shard_map/while/body/eval_jaxpr/ppermute | solution.py:13
  405.2 5.6 convolution_bitcast_fusion
  410.8 9.1 %copy.19 = f32[1280,1536]{1,0:T(8,128)} copy(f32[1280,1536]{0,1:T(8,128)} %convolution_bitcast_fusion) | data formatting | bytes 15728640
  421.3 5.8 convolution_bitcast_fusion.1
  427.0 12.1 %copy.17 = f32[1792,1536]{1,0:T(8,128)} copy(f32[1792,1536]{0,1:T(8,128)} %convolution_bitcast_fusion.1) | data formatting | bytes 22020096
  439.2 88.5 %reduce-scatter.9.cloned.1.call-done = f32[80,1536]{1,0:T(8,128)} async-done(((f32[1280,1536]{1,0:T(8,128)}), f32[80,1536]{1,0:T(8,128)}) %reduce-scatter.9.cloned.1.call-update) | async-done | bytes 491536
  527.7 2.2 copy.20
  529.9 127.7 %reduce-scatter.7.cloned.1.call-done = f32[112,1536]{1,0:T(8,128)} async-done(((f32[1792,1536]{1,0:T(8,128)}), f32[112,1536]{1,0:T(8,128)}) %reduce-scatter.7.cloned.1.call-update) | async-done | bytes 688144
  657.6 2.2 copy.18
  660.4 150.8 %all-reduce.3.cloned.1.call-done = (f32[112,1536]{0,1:T(8,128)}, f32[80,1536]{0,1:T(8,128)}) async-done(((f32[112,1536]{0,1:T(8,128)}, f32[80,1536]{0,1:T(8,128)}), (f32[112,1536]{0,1:T(8,128)}, f32[80,1536]{0,1:T(8,128)})) %all-reduce.3.cloned.1.call-update) | async-done | bytes 1179664 | tf_op jit(solution)/shard_map/psum | solution.py:124
  811.2 2.2 copy.15
  813.5 2.2 copy.16
  (205 shorter events, 88.1 us)
Async XLA Ops:
  7.2 1.6 copy-start
  7.2 5.2 copy-start.5
  7.2 520.5 %reduce-scatter.9.cloned.1.call-start = ((), (), s32[]{:S(2)}) async-start(), calls=%async_computation.3 | async-start | bytes 8355840
  7.3 5.1 copy-start.4
  12.3 2.8 copy-start.2
  12.3 2.8 copy-start.6
  13.1 1.9 copy-start.1
  22.3 15.9 %collective-permute-start.1 = (f32[128,1536]{1,0:T(8,128)S(1)}, f32[128,1536]{1,0:T(8,128)S(1)}, u32[]{:S(2)}, u32[]{:S(2)}) collective-permute-start(f32[128,1536]{1,0:T(8,128)S(1)} %convert_add_fusion.2), channel_id=1, source_target_pairs={{15,0},{0,1},{1,2},{2,3},{3,4},{4,5},{5,6},{6,7},{7,8},{8,9},{9,10... | collective-permute-start | bytes 2359304 | tf_op jit(solution)/shard_map/while/body/eval_jaxpr/ppermute | solution.py:13
  25.0 13.1 %collective-permute-start = (bf16[128,1536]{1,0:T(8,128)(2,1)S(1)}, bf16[128,1536]{1,0:T(8,128)(2,1)}, u32[]{:S(2)}, u32[]{:S(2)}) collective-permute-start(bf16[128,1536]{1,0:T(8,128)(2,1)S(1)} %copy.27), channel_id=1, source_target_pairs={{15,0},{0,1},{1,2},{2,3},{3,4},{4,5},{5,6},{6,7},{7,8},{8,9},{9,10... | collective-permute-start | bytes 1179656 | tf_op jit(solution)/shard_map/while/body/eval_jaxpr/ppermute | solution.py:13
  45.3 15.8 %collective-permute-start.1 = (f32[128,1536]{1,0:T(8,128)S(1)}, f32[128,1536]{1,0:T(8,128)S(1)}, u32[]{:S(2)}, u32[]{:S(2)}) collective-permute-start(f32[128,1536]{1,0:T(8,128)S(1)} %convert_add_fusion.2), channel_id=1, source_target_pairs={{15,0},{0,1},{1,2},{2,3},{3,4},{4,5},{5,6},{6,7},{7,8},{8,9},{9,10... | collective-permute-start | bytes 2359304 | tf_op jit(solution)/shard_map/while/body/eval_jaxpr/ppermute | solution.py:13
  48.0 13.1 %collective-permute-start = (bf16[128,1536]{1,0:T(8,128)(2,1)S(1)}, bf16[128,1536]{1,0:T(8,128)(2,1)}, u32[]{:S(2)}, u32[]{:S(2)}) collective-permute-start(bf16[128,1536]{1,0:T(8,128)(2,1)S(1)} %copy.27), channel_id=1, source_target_pairs={{15,0},{0,1},{1,2},{2,3},{3,4},{4,5},{5,6},{6,7},{7,8},{8,9},{9,10... | collective-permute-start | bytes 1179656 | tf_op jit(solution)/shard_map/while/body/eval_jaxpr/ppermute | solution.py:13
  68.3 15.8 %collective-permute-start.1 = (f32[128,1536]{1,0:T(8,128)S(1)}, f32[128,1536]{1,0:T(8,128)S(1)}, u32[]{:S(2)}, u32[]{:S(2)}) collective-permute-start(f32[128,1536]{1,0:T(8,128)S(1)} %convert_add_fusion.2), channel_id=1, source_target_pairs={{15,0},{0,1},{1,2},{2,3},{3,4},{4,5},{5,6},{6,7},{7,8},{8,9},{9,10... | collective-permute-start | bytes 2359304 | tf_op jit(solution)/shard_map/while/body/eval_jaxpr/ppermute | solution.py:13
  70.9 13.1 %collective-permute-start = (bf16[128,1536]{1,0:T(8,128)(2,1)S(1)}, bf16[128,1536]{1,0:T(8,128)(2,1)}, u32[]{:S(2)}, u32[]{:S(2)}) collective-permute-start(bf16[128,1536]{1,0:T(8,128)(2,1)S(1)} %copy.27), channel_id=1, source_target_pairs={{15,0},{0,1},{1,2},{2,3},{3,4},{4,5},{5,6},{6,7},{7,8},{8,9},{9,10... | collective-permute-start | bytes 1179656 | tf_op jit(solution)/shard_map/while/body/eval_jaxpr/ppermute | solution.py:13
  91.2 15.8 %collective-permute-start.1 = (f32[128,1536]{1,0:T(8,128)S(1)}, f32[128,1536]{1,0:T(8,128)S(1)}, u32[]{:S(2)}, u32[]{:S(2)}) collective-permute-start(f32[128,1536]{1,0:T(8,128)S(1)} %convert_add_fusion.2), channel_id=1, source_target_pairs={{15,0},{0,1},{1,2},{2,3},{3,4},{4,5},{5,6},{6,7},{7,8},{8,9},{9,10... | collective-permute-start | bytes 2359304 | tf_op jit(solution)/shard_map/while/body/eval_jaxpr/ppermute | solution.py:13
  93.9 13.1 %collective-permute-start = (bf16[128,1536]{1,0:T(8,128)(2,1)S(1)}, bf16[128,1536]{1,0:T(8,128)(2,1)}, u32[]{:S(2)}, u32[]{:S(2)}) collective-permute-start(bf16[128,1536]{1,0:T(8,128)(2,1)S(1)} %copy.27), channel_id=1, source_target_pairs={{15,0},{0,1},{1,2},{2,3},{3,4},{4,5},{5,6},{6,7},{7,8},{8,9},{9,10... | collective-permute-start | bytes 1179656 | tf_op jit(solution)/shard_map/while/body/eval_jaxpr/ppermute | solution.py:13
  114.2 15.8 %collective-permute-start.1 = (f32[128,1536]{1,0:T(8,128)S(1)}, f32[128,1536]{1,0:T(8,128)S(1)}, u32[]{:S(2)}, u32[]{:S(2)}) collective-permute-start(f32[128,1536]{1,0:T(8,128)S(1)} %convert_add_fusion.2), channel_id=1, source_target_pairs={{15,0},{0,1},{1,2},{2,3},{3,4},{4,5},{5,6},{6,7},{7,8},{8,9},{9,10... | collective-permute-start | bytes 2359304 | tf_op jit(solution)/shard_map/while/body/eval_jaxpr/ppermute | solution.py:13
  116.8 13.1 %collective-permute-start = (bf16[128,1536]{1,0:T(8,128)(2,1)S(1)}, bf16[128,1536]{1,0:T(8,128)(2,1)}, u32[]{:S(2)}, u32[]{:S(2)}) collective-permute-start(bf16[128,1536]{1,0:T(8,128)(2,1)S(1)} %copy.27), channel_id=1, source_target_pairs={{15,0},{0,1},{1,2},{2,3},{3,4},{4,5},{5,6},{6,7},{7,8},{8,9},{9,10... | collective-permute-start | bytes 1179656 | tf_op jit(solution)/shard_map/while/body/eval_jaxpr/ppermute | solution.py:13
  137.1 16.2 %collective-permute-start.1 = (f32[128,1536]{1,0:T(8,128)S(1)}, f32[128,1536]{1,0:T(8,128)S(1)}, u32[]{:S(2)}, u32[]{:S(2)}) collective-permute-start(f32[128,1536]{1,0:T(8,128)S(1)} %convert_add_fusion.2), channel_id=1, source_target_pairs={{15,0},{0,1},{1,2},{2,3},{3,4},{4,5},{5,6},{6,7},{7,8},{8,9},{9,10... | collective-permute-start | bytes 2359304 | tf_op jit(solution)/shard_map/while/body/eval_jaxpr/ppermute | solution.py:13
  139.8 13.5 %collective-permute-start = (bf16[128,1536]{1,0:T(8,128)(2,1)S(1)}, bf16[128,1536]{1,0:T(8,128)(2,1)}, u32[]{:S(2)}, u32[]{:S(2)}) collective-permute-start(bf16[128,1536]{1,0:T(8,128)(2,1)S(1)} %copy.27), channel_id=1, source_target_pairs={{15,0},{0,1},{1,2},{2,3},{3,4},{4,5},{5,6},{6,7},{7,8},{8,9},{9,10... | collective-permute-start | bytes 1179656 | tf_op jit(solution)/shard_map/while/body/eval_jaxpr/ppermute | solution.py:13
  160.4 17.9 %collective-permute-start.1 = (f32[128,1536]{1,0:T(8,128)S(1)}, f32[128,1536]{1,0:T(8,128)S(1)}, u32[]{:S(2)}, u32[]{:S(2)}) collective-permute-start(f32[128,1536]{1,0:T(8,128)S(1)} %convert_add_fusion.2), channel_id=1, source_target_pairs={{15,0},{0,1},{1,2},{2,3},{3,4},{4,5},{5,6},{6,7},{7,8},{8,9},{9,10... | collective-permute-start | bytes 2359304 | tf_op jit(solution)/shard_map/while/body/eval_jaxpr/ppermute | solution.py:13
  162.7 15.6 %collective-permute-start = (bf16[128,1536]{1,0:T(8,128)(2,1)S(1)}, bf16[128,1536]{1,0:T(8,128)(2,1)}, u32[]{:S(2)}, u32[]{:S(2)}) collective-permute-start(bf16[128,1536]{1,0:T(8,128)(2,1)S(1)} %copy.27), channel_id=1, source_target_pairs={{15,0},{0,1},{1,2},{2,3},{3,4},{4,5},{5,6},{6,7},{7,8},{8,9},{9,10... | collective-permute-start | bytes 1179656 | tf_op jit(solution)/shard_map/while/body/eval_jaxpr/ppermute | solution.py:13
  185.5 17.9 %collective-permute-start.1 = (f32[128,1536]{1,0:T(8,128)S(1)}, f32[128,1536]{1,0:T(8,128)S(1)}, u32[]{:S(2)}, u32[]{:S(2)}) collective-permute-start(f32[128,1536]{1,0:T(8,128)S(1)} %convert_add_fusion.2), channel_id=1, source_target_pairs={{15,0},{0,1},{1,2},{2,3},{3,4},{4,5},{5,6},{6,7},{7,8},{8,9},{9,10... | collective-permute-start | bytes 2359304 | tf_op jit(solution)/shard_map/while/body/eval_jaxpr/ppermute | solution.py:13
  185.7 17.7 %collective-permute-start = (bf16[128,1536]{1,0:T(8,128)(2,1)S(1)}, bf16[128,1536]{1,0:T(8,128)(2,1)}, u32[]{:S(2)}, u32[]{:S(2)}) collective-permute-start(bf16[128,1536]{1,0:T(8,128)(2,1)S(1)} %copy.27), channel_id=1, source_target_pairs={{15,0},{0,1},{1,2},{2,3},{3,4},{4,5},{5,6},{6,7},{7,8},{8,9},{9,10... | collective-permute-start | bytes 1179656 | tf_op jit(solution)/shard_map/while/body/eval_jaxpr/ppermute | solution.py:13
  210.5 17.9 %collective-permute-start.1 = (f32[128,1536]{1,0:T(8,128)S(1)}, f32[128,1536]{1,0:T(8,128)S(1)}, u32[]{:S(2)}, u32[]{:S(2)}) collective-permute-start(f32[128,1536]{1,0:T(8,128)S(1)} %convert_add_fusion.2), channel_id=1, source_target_pairs={{15,0},{0,1},{1,2},{2,3},{3,4},{4,5},{5,6},{6,7},{7,8},{8,9},{9,10... | collective-permute-start | bytes 2359304 | tf_op jit(solution)/shard_map/while/body/eval_jaxpr/ppermute | solution.py:13
  210.6 17.8 %collective-permute-start = (bf16[128,1536]{1,0:T(8,128)(2,1)S(1)}, bf16[128,1536]{1,0:T(8,128)(2,1)}, u32[]{:S(2)}, u32[]{:S(2)}) collective-permute-start(bf16[128,1536]{1,0:T(8,128)(2,1)S(1)} %copy.27), channel_id=1, source_target_pairs={{15,0},{0,1},{1,2},{2,3},{3,4},{4,5},{5,6},{6,7},{7,8},{8,9},{9,10... | collective-permute-start | bytes 1179656 | tf_op jit(solution)/shard_map/while/body/eval_jaxpr/ppermute | solution.py:13
  235.6 17.9 %collective-permute-start.1 = (f32[128,1536]{1,0:T(8,128)S(1)}, f32[128,1536]{1,0:T(8,128)S(1)}, u32[]{:S(2)}, u32[]{:S(2)}) collective-permute-start(f32[128,1536]{1,0:T(8,128)S(1)} %convert_add_fusion.2), channel_id=1, source_target_pairs={{15,0},{0,1},{1,2},{2,3},{3,4},{4,5},{5,6},{6,7},{7,8},{8,9},{9,10... | collective-permute-start | bytes 2359304 | tf_op jit(solution)/shard_map/while/body/eval_jaxpr/ppermute | solution.py:13
  235.7 17.8 %collective-permute-start = (bf16[128,1536]{1,0:T(8,128)(2,1)S(1)}, bf16[128,1536]{1,0:T(8,128)(2,1)}, u32[]{:S(2)}, u32[]{:S(2)}) collective-permute-start(bf16[128,1536]{1,0:T(8,128)(2,1)S(1)} %copy.27), channel_id=1, source_target_pairs={{15,0},{0,1},{1,2},{2,3},{3,4},{4,5},{5,6},{6,7},{7,8},{8,9},{9,10... | collective-permute-start | bytes 1179656 | tf_op jit(solution)/shard_map/while/body/eval_jaxpr/ppermute | solution.py:13
  260.6 17.9 %collective-permute-start.1 = (f32[128,1536]{1,0:T(8,128)S(1)}, f32[128,1536]{1,0:T(8,128)S(1)}, u32[]{:S(2)}, u32[]{:S(2)}) collective-permute-start(f32[128,1536]{1,0:T(8,128)S(1)} %convert_add_fusion.2), channel_id=1, source_target_pairs={{15,0},{0,1},{1,2},{2,3},{3,4},{4,5},{5,6},{6,7},{7,8},{8,9},{9,10... | collective-permute-start | bytes 2359304 | tf_op jit(solution)/shard_map/while/body/eval_jaxpr/ppermute | solution.py:13
  260.7 17.8 %collective-permute-start = (bf16[128,1536]{1,0:T(8,128)(2,1)S(1)}, bf16[128,1536]{1,0:T(8,128)(2,1)}, u32[]{:S(2)}, u32[]{:S(2)}) collective-permute-start(bf16[128,1536]{1,0:T(8,128)(2,1)S(1)} %copy.27), channel_id=1, source_target_pairs={{15,0},{0,1},{1,2},{2,3},{3,4},{4,5},{5,6},{6,7},{7,8},{8,9},{9,10... | collective-permute-start | bytes 1179656 | tf_op jit(solution)/shard_map/while/body/eval_jaxpr/ppermute | solution.py:13
  285.7 17.9 %collective-permute-start.1 = (f32[128,1536]{1,0:T(8,128)S(1)}, f32[128,1536]{1,0:T(8,128)S(1)}, u32[]{:S(2)}, u32[]{:S(2)}) collective-permute-start(f32[128,1536]{1,0:T(8,128)S(1)} %convert_add_fusion.2), channel_id=1, source_target_pairs={{15,0},{0,1},{1,2},{2,3},{3,4},{4,5},{5,6},{6,7},{7,8},{8,9},{9,10... | collective-permute-start | bytes 2359304 | tf_op jit(solution)/shard_map/while/body/eval_jaxpr/ppermute | solution.py:13
  285.8 17.8 %collective-permute-start = (bf16[128,1536]{1,0:T(8,128)(2,1)S(1)}, bf16[128,1536]{1,0:T(8,128)(2,1)}, u32[]{:S(2)}, u32[]{:S(2)}) collective-permute-start(bf16[128,1536]{1,0:T(8,128)(2,1)S(1)} %copy.27), channel_id=1, source_target_pairs={{15,0},{0,1},{1,2},{2,3},{3,4},{4,5},{5,6},{6,7},{7,8},{8,9},{9,10... | collective-permute-start | bytes 1179656 | tf_op jit(solution)/shard_map/while/body/eval_jaxpr/ppermute | solution.py:13
  310.7 17.9 %collective-permute-start.1 = (f32[128,1536]{1,0:T(8,128)S(1)}, f32[128,1536]{1,0:T(8,128)S(1)}, u32[]{:S(2)}, u32[]{:S(2)}) collective-permute-start(f32[128,1536]{1,0:T(8,128)S(1)} %convert_add_fusion.2), channel_id=1, source_target_pairs={{15,0},{0,1},{1,2},{2,3},{3,4},{4,5},{5,6},{6,7},{7,8},{8,9},{9,10... | collective-permute-start | bytes 2359304 | tf_op jit(solution)/shard_map/while/body/eval_jaxpr/ppermute | solution.py:13
  310.8 17.8 %collective-permute-start = (bf16[128,1536]{1,0:T(8,128)(2,1)S(1)}, bf16[128,1536]{1,0:T(8,128)(2,1)}, u32[]{:S(2)}, u32[]{:S(2)}) collective-permute-start(bf16[128,1536]{1,0:T(8,128)(2,1)S(1)} %copy.27), channel_id=1, source_target_pairs={{15,0},{0,1},{1,2},{2,3},{3,4},{4,5},{5,6},{6,7},{7,8},{8,9},{9,10... | collective-permute-start | bytes 1179656 | tf_op jit(solution)/shard_map/while/body/eval_jaxpr/ppermute | solution.py:13
  335.8 17.9 %collective-permute-start.1 = (f32[128,1536]{1,0:T(8,128)S(1)}, f32[128,1536]{1,0:T(8,128)S(1)}, u32[]{:S(2)}, u32[]{:S(2)}) collective-permute-start(f32[128,1536]{1,0:T(8,128)S(1)} %convert_add_fusion.2), channel_id=1, source_target_pairs={{15,0},{0,1},{1,2},{2,3},{3,4},{4,5},{5,6},{6,7},{7,8},{8,9},{9,10... | collective-permute-start | bytes 2359304 | tf_op jit(solution)/shard_map/while/body/eval_jaxpr/ppermute | solution.py:13
  335.9 17.8 %collective-permute-start = (bf16[128,1536]{1,0:T(8,128)(2,1)S(1)}, bf16[128,1536]{1,0:T(8,128)(2,1)}, u32[]{:S(2)}, u32[]{:S(2)}) collective-permute-start(bf16[128,1536]{1,0:T(8,128)(2,1)S(1)} %copy.27), channel_id=1, source_target_pairs={{15,0},{0,1},{1,2},{2,3},{3,4},{4,5},{5,6},{6,7},{7,8},{8,9},{9,10... | collective-permute-start | bytes 1179656 | tf_op jit(solution)/shard_map/while/body/eval_jaxpr/ppermute | solution.py:13
  360.8 17.9 %collective-permute-start.1 = (f32[128,1536]{1,0:T(8,128)S(1)}, f32[128,1536]{1,0:T(8,128)S(1)}, u32[]{:S(2)}, u32[]{:S(2)}) collective-permute-start(f32[128,1536]{1,0:T(8,128)S(1)} %convert_add_fusion.2), channel_id=1, source_target_pairs={{15,0},{0,1},{1,2},{2,3},{3,4},{4,5},{5,6},{6,7},{7,8},{8,9},{9,10... | collective-permute-start | bytes 2359304 | tf_op jit(solution)/shard_map/while/body/eval_jaxpr/ppermute | solution.py:13
  360.9 17.8 %collective-permute-start = (bf16[128,1536]{1,0:T(8,128)(2,1)S(1)}, bf16[128,1536]{1,0:T(8,128)(2,1)}, u32[]{:S(2)}, u32[]{:S(2)}) collective-permute-start(bf16[128,1536]{1,0:T(8,128)(2,1)S(1)} %copy.27), channel_id=1, source_target_pairs={{15,0},{0,1},{1,2},{2,3},{3,4},{4,5},{5,6},{6,7},{7,8},{8,9},{9,10... | collective-permute-start | bytes 1179656 | tf_op jit(solution)/shard_map/while/body/eval_jaxpr/ppermute | solution.py:13
  385.9 17.9 %collective-permute-start.1 = (f32[128,1536]{1,0:T(8,128)S(1)}, f32[128,1536]{1,0:T(8,128)S(1)}, u32[]{:S(2)}, u32[]{:S(2)}) collective-permute-start(f32[128,1536]{1,0:T(8,128)S(1)} %convert_add_fusion.2), channel_id=1, source_target_pairs={{15,0},{0,1},{1,2},{2,3},{3,4},{4,5},{5,6},{6,7},{7,8},{8,9},{9,10... | collective-permute-start | bytes 2359304 | tf_op jit(solution)/shard_map/while/body/eval_jaxpr/ppermute | solution.py:13
  386.0 17.8 %collective-permute-start = (bf16[128,1536]{1,0:T(8,128)(2,1)S(1)}, bf16[128,1536]{1,0:T(8,128)(2,1)}, u32[]{:S(2)}, u32[]{:S(2)}) collective-permute-start(bf16[128,1536]{1,0:T(8,128)(2,1)S(1)} %copy.27), channel_id=1, source_target_pairs={{15,0},{0,1},{1,2},{2,3},{3,4},{4,5},{5,6},{6,7},{7,8},{8,9},{9,10... | collective-permute-start | bytes 1179656 | tf_op jit(solution)/shard_map/while/body/eval_jaxpr/ppermute | solution.py:13
  419.9 1.1 copy-start.3
  419.9 237.7 %reduce-scatter.7.cloned.1.call-start = ((), (), s32[]{:S(2)}) async-start(), calls=%async_computation.2 | async-start | bytes 11698176
  439.2 372.1 %all-reduce.3.cloned.1.call-start = ((), (), s32[]{:S(2)}) async-start(), calls=%async_computation.4 | async-start | bytes 3145728 | tf_op jit(solution)/shard_map/psum | solution.py:124
Sparse Core Ops, SparseCore 0:
  420.0 107.6 reduce-scatter.8
  530.3 127.3 reduce-scatter.6
  660.3 150.8 all-reduce.2
where the time goes:
time: 836 us; the launch traced here: 822 us
  waiting for transfers between devices  586 us (70%)
  matrix products  106 us (13%)
  local copies, waits for them, and re-layouts  60.1 us (7%)
  starting transfers between devices  38.5 us (5%)
  other arithmetic  17.7 us (2%)
  between operations  13.9 us (2%)
    ppermute x32, waiting for transfers between devices, shifted(): return lax.ppermute(block, axis, route)  219 us
    unnamed x5, waiting for transfers between devices  216 us
    psum x1, waiting for transfers between devices, on_device(): grad_image, grad_text = lax.psum((grad_image, grad_text), 'dp')  151 us
    dot_general x18, matrix products, reduce_over_samples(): lax.dot_general(left, right, (((0,), (0,)), ((), ())), preferred_element_...  42.5 us
    dot_general x16, matrix products, pair_terms(): lax.dot_general(visual_normalized_vector, text_piece, (((1,), (1,)), ((),...  41.6 us
    ppermute x32, starting transfers between devices, shifted(): return lax.ppermute(block, axis, route)  38.4 us
    unnamed x20, local copies, waits for them, and re-layouts  31.2 us
    dot_general x16, matrix products, pair_terms(): jnp.dot(sigmoid_derivatives, text_piece, preferred_element_type=jnp.float32)  17.2 us
  transfers between devices with their start and end apart: 35, of which 19 were waited for; matrix products, arithmetic and copies ran while one was open for 5% of the time, Pallas kernels for 0%

commit v1 on v0

v1 whole, which is shorter than its diff:
```python
import functools

import jax
import jax.numpy as jnp
from jax import lax
from jax.experimental import pallas as pl
from jax.experimental.pallas import tpu as pltpu
from jax.sharding import PartitionSpec as P

loss_scale = 256.0
epsilon = 1e-06
MESH = pl.DeviceIdType.MESH
F32 = jnp.float32
BF16 = jnp.bfloat16


def kernel(
    total_rows, ring_z, labels, tally, sharp, shift, x_hbm, t_hbm, wv_hbm, wt_hbm,
    cost_out, gi_out, gt_out,
    wv, wt, xg, tg, zi, zt, inv_i, inv_t, u_scr, lab_i, row_rad, row_cost, txt_meta,
    slope, slope_t, stat_i, stat_t, sti_rcv, stt_rcv, stat_tot,
    gt_snd, gt_mrg, gt_rcv, gi_snd, gi_mrg, gi_rcv, d_img, d_txt, xg_t, tg_t,
    ei_snd, ei_mrg, ei_rcv, et_snd, et_mrg, et_rcv, tile, z_snd, z_rcv, y_snd, y_rcv, res, f_i, f_t,
    loc_sem, snd_sem, rcv_sem,
):
    rows = xg.shape[1]
    group = 4 * rows
    embed = zi.shape[1]
    width = embed // 4
    dp, blk = lax.axis_index("dp"), lax.axis_index("blk")
    x, q = lax.div(blk, 4), lax.rem(blk, 4)
    y, c = lax.div(q, 2), lax.rem(q, 2)
    z, yh = lax.rem(dp, ring_z), lax.div(dp, ring_z)
    xr, xl, xo = lax.rem(x + 1, 4), lax.rem(x + 3, 4), lax.rem(x + 2, 4)
    qp, qn, qd = y * 2 + 1 - c, (1 - y) * 2 + c, (1 - y) * 2 + 1 - c
    XR, XL, XO = (dp, xr * 4 + q), (dp, xl * 4 + q), (dp, xo * 4 + q)
    PT, YN, DG = (dp, x * 4 + qp), (dp, x * 4 + qn), (dp, x * 4 + qd)
    ZR = (yh * ring_z + lax.rem(z + 1, ring_z), blk)
    ZL = (yh * ring_z + lax.rem(z + ring_z - 1, ring_z), blk)
    YH = ((1 - yh) * ring_z + z, blk)

    barrier = pltpu.get_barrier_semaphore()
    peers = (XR, XL, XO, PT, YN, DG, ZR, ZL, YH)
    for peer in peers:
        pl.semaphore_signal(barrier, inc=1, device_id=peer, device_id_type=MESH)
    loc = [
        pltpu.make_async_copy(t_hbm, tg.at[x], loc_sem.at[0]),
        pltpu.make_async_copy(x_hbm, xg.at[q], loc_sem.at[1]),
        pltpu.make_async_copy(wt_hbm, wt, loc_sem.at[2]),
        pltpu.make_async_copy(wv_hbm, wv, loc_sem.at[3]),
    ]
    for copy in loc:
        copy.start()

    count = [0]
    started = []

    def slot():
        count[0] += 1
        return count[0] - 1

    def send(src, dst, sem, dev):
        copy = pltpu.make_async_remote_copy(
            src_ref=src, dst_ref=dst, send_sem=snd_sem.at[sem], recv_sem=rcv_sem.at[sem],
            device_id=dev, device_id_type=MESH,
        )
        copy.start()
        started.append(copy)

    def recv(dst, sem):
        pltpu.make_async_remote_copy(
            src_ref=dst, dst_ref=dst, send_sem=snd_sem.at[sem], recv_sem=rcv_sem.at[sem],
            device_id=XR, device_id_type=MESH,
        ).wait_recv()

    half = rows // 2
    halves = (pl.ds(0, half), pl.ds(half, half))

    pl.semaphore_wait(barrier, len(peers))
    loc[0].wait()
    t_sem = [slot() for _ in range(6)]
    send(tg.at[x, halves[0]], tg.at[x, halves[0]], t_sem[0], XR)
    send(tg.at[x, halves[1]], tg.at[x, halves[1]], t_sem[1], XL)
    send(tg.at[x, halves[1]], tg.at[x, halves[1]], t_sem[2], XR)
    send(tg.at[x, halves[0]], tg.at[x, halves[0]], t_sem[3], XL)
    loc[1].wait()
    x_sem = [slot() for _ in range(5)]
    for h in range(2):
        send(xg.at[q, halves[h]], xg.at[q, halves[h]], x_sem[h], YN)
    send(xg.at[q], xg.at[q], x_sem[2], PT)

    alive_lane = lax.broadcasted_iota(jnp.int32, (8, rows), 1)
    for k in range(4):
        cols = pl.ds(k * rows, rows)
        txt_meta[0:8, cols] = jnp.broadcast_to(labels[pl.ds(4 * k + q, 1), :], (8, rows)).astype(F32)
        txt_meta[8:16, cols] = jnp.where(alive_lane < tally[0, 4 * k + q], 1.0, 0.0)
        wide = jnp.broadcast_to(labels[pl.ds(4 * x + k, 1), :].astype(F32), (rows, rows))
        lab_i[pl.ds(k * rows, rows), :] = wide.T

    def project(source, weights, unit, inverse, k):
        def body(j, carry):
            cols = pl.ds(pl.multiple_of(j * 512, 512), 512)
            u_scr[:, cols] = jnp.dot(source[k], weights[:, cols], preferred_element_type=F32)
            return carry

        lax.fori_loop(0, embed // 512, body, 0)
        u = u_scr[...]
        inv = 1.0 / jnp.sqrt(jnp.sum(u * u, axis=1, keepdims=True) + epsilon)
        at = pl.ds(pl.multiple_of(k * rows, rows), rows)
        unit[at, :] = (u * inv).astype(BF16)
        inverse[at, :] = jnp.broadcast_to(inv, (rows, rows))

    loc[2].wait()
    project(tg, wt, zt, inv_t, x)
    recv(tg.at[xl, halves[0]], t_sem[0])
    send(tg.at[xl, halves[0]], tg.at[xl, halves[0]], t_sem[4], XR)
    recv(tg.at[xr, halves[1]], t_sem[1])
    send(tg.at[xr, halves[1]], tg.at[xr, halves[1]], t_sem[5], XL)
    loc[3].wait()
    project(xg, wv, zi, inv_i, q)
    recv(xg.at[qp], x_sem[2])
    recv(xg.at[qn, halves[0]], x_sem[0])
    send(xg.at[qn, halves[0]], xg.at[qn, halves[0]], x_sem[3], PT)
    project(xg, wv, zi, inv_i, qp)
    recv(tg.at[xl, halves[1]], t_sem[2])
    project(tg, wt, zt, inv_t, xl)
    recv(xg.at[qn, halves[1]], x_sem[1])
    send(xg.at[qn, halves[1]], xg.at[qn, halves[1]], x_sem[4], PT)
    recv(tg.at[xr, halves[0]], t_sem[3])
    project(tg, wt, zt, inv_t, xr)
    project(xg, wv, zi, inv_i, qn)
    recv(tg.at[xo, halves[0]], t_sem[4])
    recv(tg.at[xo, halves[1]], t_sem[5])
    project(tg, wt, zt, inv_t, xo)
    recv(xg.at[qd, halves[0]], x_sem[3])
    recv(xg.at[qd, halves[1]], x_sem[4])
    project(xg, wv, zi, inv_i, qd)

    scale = sharp[0]
    bias = shift[0]
    stat_t[...] = jnp.zeros_like(stat_t)

    def pair_block(k, carry):
        at = pl.ds(pl.multiple_of(k * rows, rows), rows)
        cosine = lax.dot_general(
            zi[at, :], zt[...], (((1,), (1,)), ((), ())), preferred_element_type=F32
        )
        same = lab_i[at, 0:1] == txt_meta[0:1, :]
        limit = tally[0, 4 * x + k]
        alive = lax.broadcasted_iota(jnp.int32, (rows, 1), 0) < limit
        weight = jnp.where(alive, 1.0, 0.0) * txt_meta[8:9, :]
        sign = jnp.where(same, 1.0, -1.0)
        t = -sign * (scale * cosine + bias)
        e = jnp.exp(-jnp.abs(t))
        cost = (jnp.maximum(t, 0.0) + jnp.log1p(e)) * weight
        sigmoid = jnp.where(t >= 0.0, 1.0, e) / (1.0 + e)
        s = -sign * sigmoid * weight * (loss_scale / total_rows)
        s16 = s.astype(BF16)
        slope[at, :] = s16
        s = s16.astype(F32)
        slope_t[:, at] = s.T.astype(BF16)
        along = s * cosine * scale
        row_rad[at, :] = jnp.broadcast_to(jnp.sum(along, axis=1, keepdims=True), (rows, rows))
        row_cost[at, :] = jnp.broadcast_to(jnp.sum(cost, axis=1, keepdims=True), (rows, rows))
        stat_t[...] += jnp.broadcast_to(jnp.sum(along, axis=0, keepdims=True), stat_t.shape)
        return carry

    lax.fori_loop(0, 4, pair_block, 0)
    stat_i[0:8, :] = row_rad[...].T[0:8, :]
    stat_i[8:16, :] = row_cost[...].T[0:8, :]

    def width_at(k):
        return pl.ds(pl.multiple_of(k * width, 128), width)

    def txt_part(k):
        gt_snd[k] = (
            scale * jnp.dot(slope_t[...], zi[:, width_at(k)], preferred_element_type=F32)
        ).astype(BF16)

    def img_part(k):
        gi_snd[k] = (
            scale * jnp.dot(slope[...], zt[:, width_at(k)], preferred_element_type=F32)
        ).astype(BF16)

    class RingSum:
        def __init__(self, snd, mrg, rcv):
            self.snd, self.mrg, self.rcv = snd, mrg, rcv
            h = snd.shape[1] // 2
            self.h, self.a, self.b = h, pl.ds(0, h), pl.ds(h, h)
            self.sems = [slot() for _ in range(6)]

        def far(self):
            send(self.snd.at[xo, self.a], self.rcv.at[0], self.sems[0], XR)
            send(self.snd.at[xo, self.b], self.rcv.at[1], self.sems[1], XL)

        def near(self):
            send(self.snd.at[xr, self.b], self.rcv.at[4], self.sems[4], XR)
            send(self.snd.at[xl, self.a], self.rcv.at[5], self.sems[5], XL)

        def merge(self):
            recv(self.rcv.at[0], self.sems[0])
            self.mrg[0] = (self.rcv[0].astype(F32) + self.snd[xr, self.a].astype(F32)).astype(BF16)
            send(self.mrg.at[0], self.rcv.at[2], self.sems[2], XR)
            recv(self.rcv.at[1], self.sems[1])
            self.mrg[1] = (self.rcv[1].astype(F32) + self.snd[xl, self.b].astype(F32)).astype(BF16)
            send(self.mrg.at[1], self.rcv.at[3], self.sems[3], XL)

        def arrive(self):
            for i in (4, 5, 2, 3):
                recv(self.rcv.at[i], self.sems[i])

        def top(self, start, size):
            at = pl.ds(start, size)
            return self.snd[x, at].astype(F32) + self.rcv[2, at].astype(F32) + self.rcv[5, at].astype(F32)

        def low(self, start, size):
            at = pl.ds(start, size)
            mine = self.snd[x, pl.ds(self.h + start, size)].astype(F32)
            return mine + self.rcv[3, at].astype(F32) + self.rcv[4, at].astype(F32)

    class PairSum:
        def __init__(self, snd, mrg, rcv):
            self.snd, self.mrg, self.rcv = snd, mrg, rcv
            self.sems = [slot() for _ in range(3)]

        def far(self):
            send(self.snd.at[qd], self.rcv.at[0], self.sems[0], PT)

        def near(self):
            send(self.snd.at[qp], self.rcv.at[1], self.sems[1], PT)

        def merge(self):
            recv(self.rcv.at[0], self.sems[0])
            self.mrg[...] = (self.rcv[0].astype(F32) + self.snd[qn].astype(F32)).astype(BF16)
            send(self.mrg, self.rcv.at[2], self.sems[2], YN)

        def arrive(self):
            recv(self.rcv.at[1], self.sems[1])
            recv(self.rcv.at[2], self.sems[2])

        def total(self, start, size):
            at = pl.ds(start, size)
            return self.snd[q, at].astype(F32) + self.rcv[1, at].astype(F32) + self.rcv[2, at].astype(F32)

    st_sem = [slot() for _ in range(6)]
    for i, dev in enumerate((XR, XL, XO)):
        send(stat_t, stt_rcv.at[i], st_sem[i], dev)
    for i, dev in enumerate((PT, YN, DG)):
        send(stat_i, sti_rcv.at[i], st_sem[3 + i], dev)

    txt_sum = RingSum(gt_snd, gt_mrg, gt_rcv)
    img_sum = PairSum(gi_snd, gi_mrg, gi_rcv)
    txt_part(xo)
    txt_sum.far()
    img_part(qd)
    img_sum.far()
    txt_part(xr)
    txt_part(xl)
    txt_sum.near()
    img_part(qn)
    img_sum.merge()
    img_part(qp)
    img_sum.near()
    img_part(q)
    txt_part(x)
    txt_sum.merge()
    for k in range(4):
        xg_t[:, k * rows : (k + 1) * rows] = xg[k].T

    for i in range(3):
        recv(sti_rcv.at[i], st_sem[3 + i])
    stat_tot[...] = stat_i[...] + sti_rcv[0] + sti_rcv[1] + sti_rcv[2]
    row_rad[...] = jnp.broadcast_to(stat_tot[0:1, :], (rows, group)).T
    cost_out[...] = stat_tot[8:9, pl.ds(pl.multiple_of(q * rows, rows), rows)] * (1.0 / total_rows)

    def change(out, unit, inverse, k, column, total):
        at = pl.ds(k * rows, rows)
        u = unit[at, width_at(column)].astype(F32)
        out[at, :] = ((total - u * row_rad[at, 0:1]) * inverse[at, 0:1]).astype(BF16)

    img_sum.arrive()
    for k in range(4):
        change(d_img, zi, inv_i, k, q, img_sum.total(k * rows, rows))

    part_i = RingSum(ei_snd, ei_mrg, ei_rcv)
    deep = ei_snd.shape[1]

    def image_rows(k):
        at = pl.ds(pl.multiple_of(k * deep, 64), deep)
        ei_snd[k] = jnp.dot(xg_t[at, :], d_img[...], preferred_element_type=F32).astype(BF16)

    image_rows(xo)
    part_i.far()
    image_rows(xr)
    image_rows(xl)
    part_i.near()

    for k in range(4):
        tg_t[:, k * rows : (k + 1) * rows] = tg[k].T
    for i in range(3):
        recv(stt_rcv.at[i], st_sem[i])
    txt_total = stat_t[0:1, :] + stt_rcv[0, 0:1, :] + stt_rcv[1, 0:1, :] + stt_rcv[2, 0:1, :]
    row_rad[...] = jnp.broadcast_to(txt_total, (rows, group)).T
    txt_sum.arrive()
    for k in range(2):
        change(d_txt, zt, inv_t, k, x, txt_sum.top(k * rows, rows))
    for k in range(2):
        change(d_txt, zt, inv_t, 2 + k, x, txt_sum.low(k * rows, rows))

    part_t = PairSum(et_snd, et_mrg, et_rcv)
    own_t = gt_out.shape[0]
    own_i = gi_out.shape[0]
    for k in range(4):
        part = jnp.dot(
            tg_t[4 * own_t * k : 4 * own_t * (k + 1), :], d_txt[...], preferred_element_type=F32
        ).astype(BF16)
        for owner in range(4):
            et_snd[owner, own_t * k : own_t * (k + 1), :] = part[own_t * owner : own_t * (owner + 1)]
    part_t.far()
    part_t.near()
    part_i.merge()
    image_rows(x)
    part_t.merge()

    part_i.arrive()
    tile[0 : deep // 2, :] = part_i.top(0, deep // 2)
    tile[deep // 2 : deep, :] = part_i.low(0, deep // 2)
    part_t.arrive()
    tile[deep : deep + 4 * own_t, :] = part_t.total(0, 4 * own_t)

    piece = y_snd.shape[0]
    plus, minus = ring_z // 2, (ring_z - 1) // 2

    def piece_at(k):
        return pl.ds(pl.multiple_of(lax.rem(k + ring_z, ring_z) * piece, 16), piece)

    p_sem = [slot() for _ in range(plus)]
    m_sem = [slot() for _ in range(minus)]
    for s in range(plus):
        value = tile[piece_at(z + plus - s), :]
        if s:
            recv(z_rcv.at[s - 1], p_sem[s - 1])
            value = value + z_rcv[s - 1].astype(F32)
        z_snd[s] = value.astype(BF16)
        send(z_snd.at[s], z_rcv.at[s], p_sem[s], ZR)
        if s < minus:
            value = tile[piece_at(z - (minus - s)), :]
            if s:
                recv(z_rcv.at[plus + s - 1], m_sem[s - 1])
                value = value + z_rcv[plus + s - 1].astype(F32)
            z_snd[plus + s] = value.astype(BF16)
            send(z_snd.at[plus + s], z_rcv.at[plus + s], m_sem[s], ZL)
    recv(z_rcv.at[plus + minus - 1], m_sem[minus - 1])
    recv(z_rcv.at[plus - 1], p_sem[plus - 1])
    value = tile[piece_at(z), :] + z_rcv[plus - 1].astype(F32) + z_rcv[plus + minus - 1].astype(F32)
    y_snd[...] = value.astype(BF16)
    y_sem = slot()
    send(y_snd, y_rcv, y_sem, YH)
    recv(y_rcv, y_sem)
    res[piece_at(z), :] = (y_snd[...].astype(F32) + y_rcv[...].astype(F32)).astype(BF16)
    p_sem = [slot() for _ in range(plus)]
    m_sem = [slot() for _ in range(minus)]
    for s in range(plus):
        if s:
            recv(res.at[piece_at(z - s)], p_sem[s - 1])
        send(res.at[piece_at(z - s)], res.at[piece_at(z - s)], p_sem[s], ZR)
        if s < minus:
            if s:
                recv(res.at[piece_at(z + s)], m_sem[s - 1])
            send(res.at[piece_at(z + s)], res.at[piece_at(z + s)], m_sem[s], ZL)
    recv(res.at[piece_at(z + minus)], m_sem[minus - 1])
    recv(res.at[piece_at(z - plus)], p_sem[plus - 1])

    def image_owner(k):
        return pl.ds(pl.multiple_of(k * own_i, 16), own_i)

    def text_owner(k):
        return pl.ds(pl.multiple_of(deep + k * own_t, 16), own_t)

    o_sem = [slot() for _ in range(6)]
    for i, (k, dev) in enumerate(((qd, DG), (qn, YN), (qp, PT))):
        send(res.at[image_owner(k)], f_i.at[q], o_sem[i], dev)
    for i, (k, dev) in enumerate(((xo, XO), (xr, XR), (xl, XL))):
        send(res.at[text_owner(k)], f_t.at[x], o_sem[3 + i], dev)
    gi_out[:, width_at(q)] = res[image_owner(q), :].astype(F32)
    gt_out[:, width_at(x)] = res[text_owner(x), :].astype(F32)
    for i, k in ((2, qp), (1, qn), (0, qd)):
        recv(f_i.at[k], o_sem[i])
        gi_out[:, width_at(k)] = f_i[k].astype(F32)
    for i, k in ((4, xl), (5, xr), (3, xo)):
        recv(f_t.at[k], o_sem[i])
        gt_out[:, width_at(k)] = f_t[k].astype(F32)

    for copy in started:
        copy.wait_send()


def solution(mesh):
    blocks = mesh.shape["blk"]
    ring_z = mesh.shape["dp"] // 2

    def on_device(
        visual_summary_vectors, caption_summary_vectors, pairing_identifiers, valid_sample_tally,
        visual_mapping_matrix, caption_mapping_matrix, sharpness_factor, score_shift_term,
    ):
        rows, deep_i = visual_summary_vectors.shape
        deep_t, embed = caption_mapping_matrix.shape
        group, width = 4 * rows, embed // 4
        own_i, own_t = deep_i // blocks, deep_t // blocks
        area = 4 * (own_i + own_t)
        piece = area // ring_z
        vmem = pl.BlockSpec(memory_space=pltpu.VMEM)
        smem = pl.BlockSpec(memory_space=pltpu.SMEM)
        hbm = pl.BlockSpec(memory_space=pl.ANY)
        B = lambda *shape: pltpu.VMEM(shape, BF16)
        F = lambda *shape: pltpu.VMEM(shape, F32)
        cost, grad_image, grad_text = pl.pallas_call(
            functools.partial(kernel, blocks * rows, ring_z),
            out_shape=(
                jax.ShapeDtypeStruct((1, rows), F32),
                jax.ShapeDtypeStruct((own_i, embed), F32),
                jax.ShapeDtypeStruct((own_t, embed), F32),
            ),
            in_specs=[vmem, smem, smem, smem, hbm, hbm, hbm, hbm],
            out_specs=(vmem, vmem, vmem),
            scratch_shapes=[
                B(deep_i, embed), B(deep_t, embed), B(4, rows, deep_i), B(4, rows, deep_t),
                B(group, embed), B(group, embed), F(group, rows), F(group, rows), F(rows, embed),
                F(group, rows), F(group, rows), F(group, rows), F(16, group),
                B(group, group), B(group, group), F(16, group), F(8, group),
                F(3, 16, group), F(3, 8, group), F(16, group),
                B(4, group, width), B(2, group // 2, width), B(6, group // 2, width),
                B(4, group, width), B(group, width), B(3, group, width),
                B(group, width), B(group, width), B(deep_i, group), B(deep_t, group),
                B(4, 4 * own_i, width), B(2, 2 * own_i, width), B(6, 2 * own_i, width),
                B(4, 4 * own_t, width), B(4 * own_t, width), B(3, 4 * own_t, width),
                F(area, width), B(ring_z - 1, piece, width), B(ring_z - 1, piece, width),
                B(piece, width), B(piece, width), B(area, width),
                B(4, own_i, width), B(4, own_t, width),
                pltpu.SemaphoreType.DMA((4,)),
                pltpu.SemaphoreType.DMA((64,)),
                pltpu.SemaphoreType.DMA((64,)),
            ],
            compiler_params=pltpu.CompilerParams(
                collective_id=0, has_side_effects=True, vmem_limit_bytes=60 * 1024 * 1024
            ),
            name="contrastive_step",
        )(
            pairing_identifiers.reshape(blocks, rows), valid_sample_tally, sharpness_factor, score_shift_term,
            visual_summary_vectors, caption_summary_vectors, visual_mapping_matrix, caption_mapping_matrix,
        )
        return cost.reshape(rows), grad_image, grad_text

    placed = (
        P(("dp", "blk"), None), P(("dp", "blk"), None), P("dp"), P("dp", None), P(), P(), P(), P(),
    )
    return jax.shard_map(
        on_device,
        mesh=mesh,
        in_specs=placed,
        out_specs=(P(("dp", "blk")), P("blk", None), P("blk", None)),
        check_vma=False,
    )
```

time: 836 us -> 105 us (0.13); the launches traced: 822 us -> 105 us
  waiting for transfers between devices: 586 us -> 0 us
  matrix products: 106 us -> 0 us
  Pallas kernels: 0 us -> 98.3 us
  local copies, waits for them, and re-layouts: 60.1 us -> 4.97 us
  starting transfers between devices: 38.5 us -> 0 us
  other arithmetic: 17.7 us -> 0 us
  between operations: 13.9 us -> 1.93 us
    ppermute x32 -> x0, waiting for transfers between devices: 219 us -> none  [shifted(): return lax.ppermute(block, axis, route)]
    unnamed x5 -> x0, waiting for transfers between devices: 216 us -> none
    psum x1 -> x0, waiting for transfers between devices: 151 us -> none  [on_device(): grad_image, grad_text = lax.psum((grad_image, grad_text), 'dp')]
    dot_general x52 -> x0, matrix products: 106 us -> none  [the longest x18 42.5 us: reduce_over_samples(): lax.dot_general(left, right, (((0,), (0,)), ((), ())), preferred_element_...]
    pallas_call x0 -> x1, Pallas kernels: none -> 98.3 us  [on_device(): pl.pallas_call(functools.partial(kernel, blocks * rows, ring_z), out_shap...]
    ppermute x32 -> x0, starting transfers between devices: 38.4 us -> none  [shifted(): return lax.ppermute(block, axis, route)]
    unnamed x20 -> x3, local copies, waits for them, and re-layouts: 31.2 us -> 4.97 us
    while x16 -> x0, local copies, waits for them, and re-layouts: 16 us -> none
  transfers between devices with their start and end apart: 35 -> 0, of which waited for: 19 -> 0; matrix products, arithmetic and copies ran while one was open for 5% -> 0% of each run, Pallas kernels for 0% -> 0%
where the time goes in v1:
time: 105 us
  Pallas kernels  98.3 us (94%)
  local copies, waits for them, and re-layouts  4.97 us (5%)
  between operations  1.93 us (2%)
    pallas_call x1, Pallas kernels, on_device(): pl.pallas_call(functools.partial(kernel, blocks * rows, ring_z), out_shap...  98.3 us
    unnamed x3, local copies, waits for them, and re-layouts  4.97 us

profile of v1, /device:TPU:1, one launch (start us, length us, event | category | flops | bytes accessed | tf_op | source)
XLA Modules:
  0.0 105.2 jit_solution(3319861712436101332)
XLA Ops:
  1.9 98.3 %contrastive_step.1 = (f32[1,128]{1,0:T(1,128)}, f32[112,1536]{1,0:T(8,128)}, f32[80,1536]{1,0:T(8,128)}) custom-call(s32[16,128]{1,0:T(8,128)} %bitcast.2, s32[1,16]{1,0:T(1,128)} %tally.1, f32[1]{0:T(128)S(6)} %copy.14.sharp, f32[1]{0:T(128)S(6)} %copy.15.shift, bf16[128,1792]{1,0:T(8,128)(2,1)} %x_hbm.1, bf16[128,1280]{1,0:T(8,128)(2,1)} %t_hbm.1, ...), custom_call_target="tpu_custom_call" | custom-call | tf_op jit(solution)/shard_map/contrastive_step/pallas_call | solution.py:417
  100.3 1.1 %copy.16 = f32[128]{0:T(128)} copy(f32[128]{0:T(128)} %bitcast.3) | data formatting | bytes 1024
  101.4 2.0 %copy.17 = f32[112,1536]{1,0:T(8,128)} copy(f32[112,1536]{1,0:T(8,128)} %get-tuple-element.13) | data formatting | bytes 1376256
  103.4 1.8 %copy.18 = f32[80,1536]{1,0:T(8,128)} copy(f32[80,1536]{1,0:T(8,128)} %get-tuple-element.14) | data formatting | bytes 983040

commit v2 on v1

--- a/solution.py
+++ b/solution.py
@@ -12,15 +12,17 @@
 MESH = pl.DeviceIdType.MESH
 F32 = jnp.float32
 BF16 = jnp.bfloat16
+ORDER = (0, "t", 2, 0, 2, "i", 1) + (0, 2, 1) * 7 + (0, 2, 1, 1)
 
 
 def kernel(
-    total_rows, ring_z, labels, tally, sharp, shift, x_hbm, t_hbm, wv_hbm, wt_hbm,
-    cost_out, gi_out, gt_out,
+    total_rows, ring_z, lab_hbm, tal_hbm, sha_hbm, shi_hbm, x_hbm, t_hbm, wv_hbm, wt_hbm,
+    cost_out, f_i, f_t,
+    labels, tally, sharp, shift,
     wv, wt, xg, tg, zi, zt, inv_i, inv_t, u_scr, lab_i, row_rad, row_cost, txt_meta,
     slope, slope_t, stat_i, stat_t, sti_rcv, stt_rcv, stat_tot,
     gt_snd, gt_mrg, gt_rcv, gi_snd, gi_mrg, gi_rcv, d_img, d_txt, xg_t, tg_t,
-    ei_snd, ei_mrg, ei_rcv, et_snd, et_mrg, et_rcv, tile, z_snd, z_rcv, y_snd, y_rcv, res, f_i, f_t,
+    e0_snd, e0_mrg, e0_rcv, e1_snd, e1_mrg, e1_rcv, et_snd, et_mrg, et_rcv, tile, z_snd, z_rcv, y_snd, y_rcv, res,
     loc_sem, snd_sem, rcv_sem,
 ):
     rows = xg.shape[1]
@@ -48,6 +50,10 @@
         pltpu.make_async_copy(x_hbm, xg.at[q], loc_sem.at[1]),
         pltpu.make_async_copy(wt_hbm, wt, loc_sem.at[2]),
         pltpu.make_async_copy(wv_hbm, wv, loc_sem.at[3]),
+        pltpu.make_async_copy(lab_hbm, labels, loc_sem.at[4]),
+        pltpu.make_async_copy(tal_hbm, tally, loc_sem.at[5]),
+        pltpu.make_async_copy(sha_hbm, sharp, loc_sem.at[6]),
+        pltpu.make_async_copy(shi_hbm, shift, loc_sem.at[7]),
     ]
     for copy in loc:
         copy.start()
@@ -89,6 +95,8 @@
         send(xg.at[q, halves[h]], xg.at[q, halves[h]], x_sem[h], YN)
     send(xg.at[q], xg.at[q], x_sem[2], PT)
 
+    for copy in loc[4:]:
+        copy.wait()
     alive_lane = lax.broadcasted_iota(jnp.int32, (8, rows), 1)
     for k in range(4):
         cols = pl.ds(k * rows, rows)
@@ -282,18 +290,26 @@
     for k in range(4):
         change(d_img, zi, inv_i, k, q, img_sum.total(k * rows, rows))
 
-    part_i = RingSum(ei_snd, ei_mrg, ei_rcv)
-    deep = ei_snd.shape[1]
+    own_i, own_t = 16 * f_i.shape[1], 16 * f_t.shape[1]
+    cut_i, cut_t = own_i - 48, own_t - 64
+    part_0 = RingSum(e0_snd, e0_mrg, e0_rcv)
+    part_1 = RingSum(e1_snd, e1_mrg, e1_rcv)
+    deep = 4 * own_i
 
     def image_rows(k):
         at = pl.ds(pl.multiple_of(k * deep, 64), deep)
-        ei_snd[k] = jnp.dot(xg_t[at, :], d_img[...], preferred_element_type=F32).astype(BF16)
+        part = jnp.dot(xg_t[at, :], d_img[...], preferred_element_type=F32).astype(BF16)
+        for owner in range(4):
+            lo, mid, hi = own_i * owner, own_i * owner + cut_i, own_i * (owner + 1)
+            e0_snd[k, cut_i * owner : cut_i * (owner + 1), :] = part[lo:mid]
+            e1_snd[k, 48 * owner : 48 * (owner + 1), :] = part[mid:hi]
 
     image_rows(xo)
-    part_i.far()
+    part_0.far()
     image_rows(xr)
     image_rows(xl)
-    part_i.near()
+    part_0.near()
+    part_1.far()
 
     for k in range(4):
         tg_t[:, k * rows : (k + 1) * rows] = tg[k].T
@@ -308,91 +324,135 @@
         change(d_txt, zt, inv_t, 2 + k, x, txt_sum.low(k * rows, rows))
 
     part_t = PairSum(et_snd, et_mrg, et_rcv)
-    own_t = gt_out.shape[0]
-    own_i = gi_out.shape[0]
     for k in range(4):
         part = jnp.dot(
             tg_t[4 * own_t * k : 4 * own_t * (k + 1), :], d_txt[...], preferred_element_type=F32
         ).astype(BF16)
         for owner in range(4):
-            et_snd[owner, own_t * k : own_t * (k + 1), :] = part[own_t * owner : own_t * (owner + 1)]
+            lo, mid, hi = own_t * owner, own_t * owner + cut_t, own_t * (owner + 1)
+            et_snd[owner, cut_t * k : cut_t * (k + 1), :] = part[lo:mid]
+            et_snd[owner, 4 * cut_t + 64 * k : 4 * cut_t + 64 * (k + 1), :] = part[mid:hi]
     part_t.far()
     part_t.near()
-    part_i.merge()
+    part_0.merge()
+    part_1.near()
     image_rows(x)
     part_t.merge()
-
-    part_i.arrive()
-    tile[0 : deep // 2, :] = part_i.top(0, deep // 2)
-    tile[deep // 2 : deep, :] = part_i.low(0, deep // 2)
-    part_t.arrive()
-    tile[deep : deep + 4 * own_t, :] = part_t.total(0, 4 * own_t)
-
-    piece = y_snd.shape[0]
+    part_1.merge()
+
     plus, minus = ring_z // 2, (ring_z - 1) // 2
-
-    def piece_at(k):
-        return pl.ds(pl.multiple_of(lax.rem(k + ring_z, ring_z) * piece, 16), piece)
-
-    p_sem = [slot() for _ in range(plus)]
-    m_sem = [slot() for _ in range(minus)]
-    for s in range(plus):
-        value = tile[piece_at(z + plus - s), :]
-        if s:
-            recv(z_rcv.at[s - 1], p_sem[s - 1])
-            value = value + z_rcv[s - 1].astype(F32)
-        z_snd[s] = value.astype(BF16)
-        send(z_snd.at[s], z_rcv.at[s], p_sem[s], ZR)
-        if s < minus:
-            value = tile[piece_at(z - (minus - s)), :]
+    own_sem = [slot() for _ in range(12)]
+
+    def units(value):
+        return value.reshape(-1, 16, width)
+
+    def at_z(k):
+        return pl.ds(2 * lax.rem(k + ring_z, ring_z), 2)
+
+    def to_owners(p):
+        plans = {
+            0: ((f_i, q, 4, 0, 0, ((qd, DG), (qn, YN), (qp, PT)), 0),),
+            1: (
+                (f_i, q, 3, 0, 4, ((qd, DG), (qn, YN), (qp, PT)), 3),
+                (f_t, x, 1, 12, 0, ((xo, XO), (xr, XR), (xl, XL)), 6),
+            ),
+            2: ((f_t, x, 4, 0, 1, ((xo, XO), (xr, XR), (xl, XL)), 9),),
+        }[p]
+        for out, mine, size, base, at, dests, sem in plans:
+            for i, (k, dev) in enumerate(dests):
+                send(
+                    res.at[p, pl.ds(base + size * k, size)], out.at[mine, pl.ds(at, size)],
+                    own_sem[sem + i], dev,
+                )
+            copy = pltpu.make_async_copy(
+                res.at[p, pl.ds(base + size * mine, size)], out.at[mine, pl.ds(at, size)],
+                loc_sem.at[8 + sem // 3],
+            )
+            copy.start()
+            kept.append(copy)
+
+    kept = []
+
+    def chain(p):
+        p_sem = [slot() for _ in range(plus)]
+        m_sem = [slot() for _ in range(minus)]
+        for s in range(plus):
+            value = tile[p, at_z(z + plus - s)]
             if s:
-                recv(z_rcv.at[plus + s - 1], m_sem[s - 1])
-                value = value + z_rcv[plus + s - 1].astype(F32)
-            z_snd[plus + s] = value.astype(BF16)
-            send(z_snd.at[plus + s], z_rcv.at[plus + s], m_sem[s], ZL)
-    recv(z_rcv.at[plus + minus - 1], m_sem[minus - 1])
-    recv(z_rcv.at[plus - 1], p_sem[plus - 1])
-    value = tile[piece_at(z), :] + z_rcv[plus - 1].astype(F32) + z_rcv[plus + minus - 1].astype(F32)
-    y_snd[...] = value.astype(BF16)
-    y_sem = slot()
-    send(y_snd, y_rcv, y_sem, YH)
-    recv(y_rcv, y_sem)
-    res[piece_at(z), :] = (y_snd[...].astype(F32) + y_rcv[...].astype(F32)).astype(BF16)
-    p_sem = [slot() for _ in range(plus)]
-    m_sem = [slot() for _ in range(minus)]
-    for s in range(plus):
-        if s:
-            recv(res.at[piece_at(z - s)], p_sem[s - 1])
-        send(res.at[piece_at(z - s)], res.at[piece_at(z - s)], p_sem[s], ZR)
-        if s < minus:
+                recv(z_rcv.at[p, s - 1], p_sem[s - 1])
+                value = value + z_rcv[p, s - 1].astype(F32)
+            z_snd[p, s] = value.astype(BF16)
+            send(z_snd.at[p, s], z_rcv.at[p, s], p_sem[s], ZR)
+            if s < minus:
+                value = tile[p, at_z(z - (minus - s))]
+                if s:
+                    recv(z_rcv.at[p, plus + s - 1], m_sem[s - 1])
+                    value = value + z_rcv[p, plus + s - 1].astype(F32)
+                z_snd[p, plus + s] = value.astype(BF16)
+                send(z_snd.at[p, plus + s], z_rcv.at[p, plus + s], m_sem[s], ZL)
+            yield
+        recv(z_rcv.at[p, plus + minus - 1], m_sem[minus - 1])
+        recv(z_rcv.at[p, plus - 1], p_sem[plus - 1])
+        value = tile[p, at_z(z)] + z_rcv[p, plus - 1].astype(F32) + z_rcv[p, plus + minus - 1].astype(F32)
+        y_snd[p] = value.astype(BF16)
+        y_sem = slot()
+        send(y_snd.at[p], y_rcv.at[p], y_sem, YH)
+        yield
+        recv(y_rcv.at[p], y_sem)
+        res[p, at_z(z)] = (y_snd[p].astype(F32) + y_rcv[p].astype(F32)).astype(BF16)
+        p_sem = [slot() for _ in range(plus)]
+        m_sem = [slot() for _ in range(minus)]
+        for s in range(plus):
             if s:
-                recv(res.at[piece_at(z + s)], m_sem[s - 1])
-            send(res.at[piece_at(z + s)], res.at[piece_at(z + s)], m_sem[s], ZL)
-    recv(res.at[piece_at(z + minus)], m_sem[minus - 1])
-    recv(res.at[piece_at(z - plus)], p_sem[plus - 1])
-
-    def image_owner(k):
-        return pl.ds(pl.multiple_of(k * own_i, 16), own_i)
-
-    def text_owner(k):
-        return pl.ds(pl.multiple_of(deep + k * own_t, 16), own_t)
-
-    o_sem = [slot() for _ in range(6)]
-    for i, (k, dev) in enumerate(((qd, DG), (qn, YN), (qp, PT))):
-        send(res.at[image_owner(k)], f_i.at[q], o_sem[i], dev)
-    for i, (k, dev) in enumerate(((xo, XO), (xr, XR), (xl, XL))):
-        send(res.at[text_owner(k)], f_t.at[x], o_sem[3 + i], dev)
-    gi_out[:, width_at(q)] = res[image_owner(q), :].astype(F32)
-    gt_out[:, width_at(x)] = res[text_owner(x), :].astype(F32)
+                recv(res.at[p, at_z(z - s)], p_sem[s - 1])
+            send(res.at[p, at_z(z - s)], res.at[p, at_z(z - s)], p_sem[s], ZR)
+            if s < minus:
+                if s:
+                    recv(res.at[p, at_z(z + s)], m_sem[s - 1])
+                send(res.at[p, at_z(z + s)], res.at[p, at_z(z + s)], m_sem[s], ZL)
+            yield
+        recv(res.at[p, at_z(z + minus)], m_sem[minus - 1])
+        recv(res.at[p, at_z(z - plus)], p_sem[plus - 1])
+        to_owners(p)
+        yield
+
+    chains = [chain(p) for p in range(3)]
+    part_0.arrive()
+    n0, n1 = 4 * cut_i, 4 * 48
+    tile[0, 0 : n0 // 32] = units(part_0.top(0, n0 // 2))
+    tile[0, n0 // 32 : n0 // 16] = units(part_0.low(0, n0 // 2))
+    for p in ORDER:
+        if p == "t":
+            part_t.arrive()
+            tile[1, n1 // 16 : 16] = units(part_t.total(0, 4 * cut_t))
+            tile[2] = units(part_t.total(4 * cut_t, 256))
+        elif p == "i":
+            part_1.arrive()
+            tile[1, 0 : n1 // 32] = units(part_1.top(0, n1 // 2))
+            tile[1, n1 // 32 : n1 // 16] = units(part_1.low(0, n1 // 2))
+        else:
+            next(chains[p])
+
     for i, k in ((2, qp), (1, qn), (0, qd)):
-        recv(f_i.at[k], o_sem[i])
-        gi_out[:, width_at(k)] = f_i[k].astype(F32)
-    for i, k in ((4, xl), (5, xr), (3, xo)):
-        recv(f_t.at[k], o_sem[i])
-        gt_out[:, width_at(k)] = f_t[k].astype(F32)
+        recv(f_i.at[k, pl.ds(0, 4)], own_sem[i])
+        recv(f_i.at[k, pl.ds(4, 3)], own_sem[3 + i])
+    for i, k in ((1, xl), (2, xr), (0, xo)):
+        recv(f_t.at[k, pl.ds(0, 1)], own_sem[6 + i])
+        recv(f_t.at[k, pl.ds(1, 4)], own_sem[9 + i])
+    for copy in kept:
+        copy.wait()
 
     for copy in started:
         copy.wait_send()
+
+
+def widen(cost, images, texts, cost_out, image_out, text_out):
+    width = images.shape[-1]
+    cost_out[...] = cost[...]
+    for k in range(4):
+        cols = pl.ds(k * width, width)
+        image_out[:, cols] = images[k].reshape(-1, width).astype(F32)
+        text_out[:, cols] = texts[k].reshape(-1, width).astype(F32)
 
 
 def solution(mesh):
@@ -407,23 +467,23 @@
         deep_t, embed = caption_mapping_matrix.shape
         group, width = 4 * rows, embed // 4
         own_i, own_t = deep_i // blocks, deep_t // blocks
-        area = 4 * (own_i + own_t)
-        piece = area // ring_z
         vmem = pl.BlockSpec(memory_space=pltpu.VMEM)
-        smem = pl.BlockSpec(memory_space=pltpu.SMEM)
         hbm = pl.BlockSpec(memory_space=pl.ANY)
         B = lambda *shape: pltpu.VMEM(shape, BF16)
         F = lambda *shape: pltpu.VMEM(shape, F32)
-        cost, grad_image, grad_text = pl.pallas_call(
+        n0, n1, nt = 4 * (own_i - 48), 4 * 48, 4 * own_t
+        cost, images, texts = pl.pallas_call(
             functools.partial(kernel, blocks * rows, ring_z),
             out_shape=(
                 jax.ShapeDtypeStruct((1, rows), F32),
-                jax.ShapeDtypeStruct((own_i, embed), F32),
-                jax.ShapeDtypeStruct((own_t, embed), F32),
+                jax.ShapeDtypeStruct((4, own_i // 16, 16, width), BF16),
+                jax.ShapeDtypeStruct((4, own_t // 16, 16, width), BF16),
             ),
-            in_specs=[vmem, smem, smem, smem, hbm, hbm, hbm, hbm],
-            out_specs=(vmem, vmem, vmem),
+            in_specs=[hbm] * 8,
+            out_specs=(vmem, hbm, hbm),
             scratch_shapes=[
+                pltpu.VMEM((blocks, rows), jnp.int32), pltpu.SMEM((1, blocks), jnp.int32),
+                pltpu.SMEM((1,), F32), pltpu.SMEM((1,), F32),
                 B(deep_i, embed), B(deep_t, embed), B(4, rows, deep_i), B(4, rows, deep_t),
                 B(group, embed), B(group, embed), F(group, rows), F(group, rows), F(rows, embed),
                 F(group, rows), F(group, rows), F(group, rows), F(16, group),
@@ -432,14 +492,14 @@
                 B(4, group, width), B(2, group // 2, width), B(6, group // 2, width),
                 B(4, group, width), B(group, width), B(3, group, width),
                 B(group, width), B(group, width), B(deep_i, group), B(deep_t, group),
-                B(4, 4 * own_i, width), B(2, 2 * own_i, width), B(6, 2 * own_i, width),
-                B(4, 4 * own_t, width), B(4 * own_t, width), B(3, 4 * own_t, width),
-                F(area, width), B(ring_z - 1, piece, width), B(ring_z - 1, piece, width),
-                B(piece, width), B(piece, width), B(area, width),
-                B(4, own_i, width), B(4, own_t, width),
-                pltpu.SemaphoreType.DMA((4,)),
-                pltpu.SemaphoreType.DMA((64,)),
-                pltpu.SemaphoreType.DMA((64,)),
+                B(4, n0, width), B(2, n0 // 2, width), B(6, n0 // 2, width),
+                B(4, n1, width), B(2, n1 // 2, width), B(6, n1 // 2, width),
+                B(4, nt, width), B(nt, width), B(3, nt, width),
+                F(3, 16, 16, width), B(3, ring_z - 1, 2, 16, width), B(3, ring_z - 1, 2, 16, width),
+                B(3, 2, 16, width), B(3, 2, 16, width), B(3, 16, 16, width),
+                pltpu.SemaphoreType.DMA((12,)),
+                pltpu.SemaphoreType.DMA((128,)),
+                pltpu.SemaphoreType.DMA((128,)),
             ],
             compiler_params=pltpu.CompilerParams(
                 collective_id=0, has_side_effects=True, vmem_limit_bytes=60 * 1024 * 1024
@@ -449,6 +509,17 @@
             pairing_identifiers.reshape(blocks, rows), valid_sample_tally, sharpness_factor, score_shift_term,
             visual_summary_vectors, caption_summary_vectors, visual_mapping_matrix, caption_mapping_matrix,
         )
+        cost, grad_image, grad_text = pl.pallas_call(
+            widen,
+            out_shape=(
+                jax.ShapeDtypeStruct((1, rows), F32),
+                jax.ShapeDtypeStruct((own_i, embed), F32),
+                jax.ShapeDtypeStruct((own_t, embed), F32),
+            ),
+            in_specs=[vmem] * 3,
+            out_specs=(vmem,) * 3,
+            name="widen",
+        )(cost, images, texts)
         return cost.reshape(rows), grad_image, grad_text
 
     placed = (

time: 105 us -> 97.9 us (0.932)
  local copies, waits for them, and re-layouts: 4.97 us -> 0 us
  Pallas kernels: 98.3 us -> 95.8 us
    unnamed x3 -> x0, local copies, waits for them, and re-layouts: 4.97 us -> none
    pallas_call x1, Pallas kernels: 98.3 us -> 93.7 us  [on_device(): pl.pallas_call(functools.partial(kernel, blocks * rows, ring_z), out_shap...]
    pallas_call x0 -> x1, Pallas kernels: none -> 2.11 us  [on_device(): pl.pallas_call(widen, out_shape=(jax.ShapeDtypeStruct((1, rows), F32), ja...]
where the time goes in v2:
time: 97.9 us; the launch traced here: 97.7 us
  Pallas kernels  95.8 us (98%)
  between operations  1.93 us (2%)
    pallas_call x1, Pallas kernels, on_device(): pl.pallas_call(functools.partial(kernel, blocks * rows, ring_z), out_shap...  93.7 us
    pallas_call x1, Pallas kernels, on_device(): pl.pallas_call(widen, out_shape=(jax.ShapeDtypeStruct((1, rows), F32), ja...  2.11 us

profile of v2, /device:TPU:1, one launch (start us, length us, event | category | flops | bytes accessed | tf_op | source)
XLA Modules:
  0.0 97.7 jit_solution(11476768031546519986)
XLA Ops:
  1.9 93.7 %contrastive_step.1 = (f32[1,128]{1,0:T(1,128)}, bf16[4,7,16,384]{3,2,1,0:T(8,128)(2,1)}, bf16[4,5,16,384]{3,2,1,0:T(8,128)(2,1)}) custom-call(s32[16,128]{1,0:T(8,128)} %bitcast.2, s32[1,16]{1,0:T(1,128)} %tal_hbm.1, f32[1]{0:T(128)S(6)} %copy.11.sha_hbm, f32[1]{0:T(128)S(6)} %copy.12.shi_hbm, bf16[128,1792]{1,0:T(8,128)(2,1)} %x_hbm.1, ...), custom_call_target="tpu_custom_call" | custom-call | tf_op jit(solution)/shard_map/contrastive_step/pallas_call | solution.py:475
  95.6 2.1 %widen.1 = (f32[1,128]{1,0:T(1,128)}, f32[112,1536]{1,0:T(8,128)}, f32[80,1536]{1,0:T(8,128)}) custom-call(f32[1,128]{1,0:T(1,128)} %get-tuple-element.9.cost, bf16[4,7,16,384]{3,2,1,0:T(8,128)(2,1)} %get-tuple-element.10.images, bf16[4,5,16,384]{3,2,1,0:T(8,128)(2,1)} %get-tuple-element.11.texts), custom_call_target="tpu_custom_call" | custom-call | tf_op jit(solution)/shard_map/widen/pallas_call | solution.py:512

commit v3 on v2

--- a/solution.py
+++ b/solution.py
@@ -12,14 +12,14 @@
 MESH = pl.DeviceIdType.MESH
 F32 = jnp.float32
 BF16 = jnp.bfloat16
-ORDER = (0, "t", 2, 0, 2, "i", 1) + (0, 2, 1) * 7 + (0, 2, 1, 1)
+ORDER = (0, "t", 2, "i", 1) + (0, 2, 1) * 5
 
 
 def kernel(
     total_rows, ring_z, lab_hbm, tal_hbm, sha_hbm, shi_hbm, x_hbm, t_hbm, wv_hbm, wt_hbm,
     cost_out, f_i, f_t,
     labels, tally, sharp, shift,
-    wv, wt, xg, tg, zi, zt, inv_i, inv_t, u_scr, lab_i, row_rad, row_cost, txt_meta,
+    wv, wt, xg, tg, zi, zt, inv_i, inv_t, u_scr, lab_i, row_alive, row_rad, row_cost, col_rad, txt_meta,
     slope, slope_t, stat_i, stat_t, sti_rcv, stt_rcv, stat_tot,
     gt_snd, gt_mrg, gt_rcv, gi_snd, gi_mrg, gi_rcv, d_img, d_txt, xg_t, tg_t,
     e0_snd, e0_mrg, e0_rcv, e1_snd, e1_mrg, e1_rcv, et_snd, et_mrg, et_rcv, tile, z_snd, z_rcv, y_snd, y_rcv, res,
@@ -35,14 +35,15 @@
     z, yh = lax.rem(dp, ring_z), lax.div(dp, ring_z)
     xr, xl, xo = lax.rem(x + 1, 4), lax.rem(x + 3, 4), lax.rem(x + 2, 4)
     qp, qn, qd = y * 2 + 1 - c, (1 - y) * 2 + c, (1 - y) * 2 + 1 - c
+    text_order = (x, xr, xl, xo)
+    image_order = (q, qp, qn, qd)
     XR, XL, XO = (dp, xr * 4 + q), (dp, xl * 4 + q), (dp, xo * 4 + q)
     PT, YN, DG = (dp, x * 4 + qp), (dp, x * 4 + qn), (dp, x * 4 + qd)
-    ZR = (yh * ring_z + lax.rem(z + 1, ring_z), blk)
-    ZL = (yh * ring_z + lax.rem(z + ring_z - 1, ring_z), blk)
+    Z = {k: (yh * ring_z + lax.rem(z + k + ring_z, ring_z), blk) for k in (1, -1, 2, -2)}
     YH = ((1 - yh) * ring_z + z, blk)
 
     barrier = pltpu.get_barrier_semaphore()
-    peers = (XR, XL, XO, PT, YN, DG, ZR, ZL, YH)
+    peers = (XR, XL, XO, PT, YN, DG, YH, *Z.values())
     for peer in peers:
         pl.semaphore_signal(barrier, inc=1, device_id=peer, device_id_type=MESH)
     loc = [
@@ -100,12 +101,14 @@
     alive_lane = lax.broadcasted_iota(jnp.int32, (8, rows), 1)
     for k in range(4):
         cols = pl.ds(k * rows, rows)
-        txt_meta[0:8, cols] = jnp.broadcast_to(labels[pl.ds(4 * k + q, 1), :], (8, rows)).astype(F32)
-        txt_meta[8:16, cols] = jnp.where(alive_lane < tally[0, 4 * k + q], 1.0, 0.0)
-        wide = jnp.broadcast_to(labels[pl.ds(4 * x + k, 1), :].astype(F32), (rows, rows))
+        block = 4 * text_order[k] + q
+        txt_meta[0:8, cols] = jnp.broadcast_to(labels[pl.ds(block, 1), :], (8, rows)).astype(F32)
+        txt_meta[8:16, cols] = jnp.where(alive_lane < tally[0, block], 1.0, 0.0)
+        block = 4 * x + image_order[k]
+        wide = jnp.broadcast_to(labels[pl.ds(block, 1), :].astype(F32), (rows, rows))
         lab_i[pl.ds(k * rows, rows), :] = wide.T
 
-    def project(source, weights, unit, inverse, k):
+    def project(source, weights, unit, inverse, k, role):
         def body(j, carry):
             cols = pl.ds(pl.multiple_of(j * 512, 512), 512)
             u_scr[:, cols] = jnp.dot(source[k], weights[:, cols], preferred_element_type=F32)
@@ -114,49 +117,20 @@
         lax.fori_loop(0, embed // 512, body, 0)
         u = u_scr[...]
         inv = 1.0 / jnp.sqrt(jnp.sum(u * u, axis=1, keepdims=True) + epsilon)
-        at = pl.ds(pl.multiple_of(k * rows, rows), rows)
+        at = pl.ds(role * rows, rows)
         unit[at, :] = (u * inv).astype(BF16)
         inverse[at, :] = jnp.broadcast_to(inv, (rows, rows))
 
-    loc[2].wait()
-    project(tg, wt, zt, inv_t, x)
-    recv(tg.at[xl, halves[0]], t_sem[0])
-    send(tg.at[xl, halves[0]], tg.at[xl, halves[0]], t_sem[4], XR)
-    recv(tg.at[xr, halves[1]], t_sem[1])
-    send(tg.at[xr, halves[1]], tg.at[xr, halves[1]], t_sem[5], XL)
-    loc[3].wait()
-    project(xg, wv, zi, inv_i, q)
-    recv(xg.at[qp], x_sem[2])
-    recv(xg.at[qn, halves[0]], x_sem[0])
-    send(xg.at[qn, halves[0]], xg.at[qn, halves[0]], x_sem[3], PT)
-    project(xg, wv, zi, inv_i, qp)
-    recv(tg.at[xl, halves[1]], t_sem[2])
-    project(tg, wt, zt, inv_t, xl)
-    recv(xg.at[qn, halves[1]], x_sem[1])
-    send(xg.at[qn, halves[1]], xg.at[qn, halves[1]], x_sem[4], PT)
-    recv(tg.at[xr, halves[0]], t_sem[3])
-    project(tg, wt, zt, inv_t, xr)
-    project(xg, wv, zi, inv_i, qn)
-    recv(tg.at[xo, halves[0]], t_sem[4])
-    recv(tg.at[xo, halves[1]], t_sem[5])
-    project(tg, wt, zt, inv_t, xo)
-    recv(xg.at[qd, halves[0]], x_sem[3])
-    recv(xg.at[qd, halves[1]], x_sem[4])
-    project(xg, wv, zi, inv_i, qd)
-
     scale = sharp[0]
     bias = shift[0]
-    stat_t[...] = jnp.zeros_like(stat_t)
-
-    def pair_block(k, carry):
-        at = pl.ds(pl.multiple_of(k * rows, rows), rows)
+
+    def pair(first, n_rows, left, n_cols):
+        at, cols = pl.ds(first, n_rows), pl.ds(left, n_cols)
         cosine = lax.dot_general(
-            zi[at, :], zt[...], (((1,), (1,)), ((), ())), preferred_element_type=F32
+            zi[at, :], zt[cols, :], (((1,), (1,)), ((), ())), preferred_element_type=F32
         )
-        same = lab_i[at, 0:1] == txt_meta[0:1, :]
-        limit = tally[0, 4 * x + k]
-        alive = lax.broadcasted_iota(jnp.int32, (rows, 1), 0) < limit
-        weight = jnp.where(alive, 1.0, 0.0) * txt_meta[8:9, :]
+        same = lab_i[at, 0:1] == txt_meta[0:1, cols]
+        weight = row_alive[at, 0:1] * txt_meta[8:9, cols]
         sign = jnp.where(same, 1.0, -1.0)
         t = -sign * (scale * cosine + bias)
         e = jnp.exp(-jnp.abs(t))
@@ -164,31 +138,73 @@
         sigmoid = jnp.where(t >= 0.0, 1.0, e) / (1.0 + e)
         s = -sign * sigmoid * weight * (loss_scale / total_rows)
         s16 = s.astype(BF16)
-        slope[at, :] = s16
+        slope[at, cols] = s16
         s = s16.astype(F32)
-        slope_t[:, at] = s.T.astype(BF16)
+        slope_t[cols, at] = s.T.astype(BF16)
         along = s * cosine * scale
-        row_rad[at, :] = jnp.broadcast_to(jnp.sum(along, axis=1, keepdims=True), (rows, rows))
-        row_cost[at, :] = jnp.broadcast_to(jnp.sum(cost, axis=1, keepdims=True), (rows, rows))
-        stat_t[...] += jnp.broadcast_to(jnp.sum(along, axis=0, keepdims=True), stat_t.shape)
-        return carry
-
-    lax.fori_loop(0, 4, pair_block, 0)
-    stat_i[0:8, :] = row_rad[...].T[0:8, :]
-    stat_i[8:16, :] = row_cost[...].T[0:8, :]
+        row_rad[at, :] += jnp.broadcast_to(jnp.sum(along, axis=1, keepdims=True), (n_rows, rows))
+        row_cost[at, :] += jnp.broadcast_to(jnp.sum(cost, axis=1, keepdims=True), (n_rows, rows))
+        col_rad[0:8, cols] += jnp.broadcast_to(jnp.sum(along, axis=0, keepdims=True), (8, n_cols))
+
+    row_rad[...] = jnp.zeros_like(row_rad)
+    row_cost[...] = jnp.zeros_like(row_cost)
+    col_rad[...] = jnp.zeros_like(col_rad)
+    down = lax.broadcasted_iota(jnp.int32, (rows, rows), 0)
+    for k in range(4):
+        row_alive[k * rows : (k + 1) * rows, :] = jnp.where(down < tally[0, 4 * x + image_order[k]], 1.0, 0.0)
+
+    loc[2].wait()
+    project(tg, wt, zt, inv_t, x, 0)
+    recv(tg.at[xl, halves[0]], t_sem[0])
+    send(tg.at[xl, halves[0]], tg.at[xl, halves[0]], t_sem[4], XR)
+    recv(tg.at[xr, halves[1]], t_sem[1])
+    send(tg.at[xr, halves[1]], tg.at[xr, halves[1]], t_sem[5], XL)
+    loc[3].wait()
+    project(xg, wv, zi, inv_i, q, 0)
+    recv(xg.at[qp], x_sem[2])
+    recv(xg.at[qn, halves[0]], x_sem[0])
+    send(xg.at[qn, halves[0]], xg.at[qn, halves[0]], x_sem[3], PT)
+    project(xg, wv, zi, inv_i, qp, 1)
+    recv(tg.at[xr, halves[0]], t_sem[3])
+    project(tg, wt, zt, inv_t, xr, 1)
+    recv(xg.at[qn, halves[1]], x_sem[1])
+    send(xg.at[qn, halves[1]], xg.at[qn, halves[1]], x_sem[4], PT)
+    recv(tg.at[xl, halves[1]], t_sem[2])
+    project(tg, wt, zt, inv_t, xl, 2)
+    project(xg, wv, zi, inv_i, qn, 2)
+    for k in range(3):
+        pair(k * rows, rows, 0, 3 * rows)
+    recv(tg.at[xo, halves[0]], t_sem[4])
+    recv(tg.at[xo, halves[1]], t_sem[5])
+    project(tg, wt, zt, inv_t, xo, 3)
+    pair(0, 3 * rows, 3 * rows, rows)
+    recv(xg.at[qd, halves[0]], x_sem[3])
+    recv(xg.at[qd, halves[1]], x_sem[4])
+    project(xg, wv, zi, inv_i, qd, 3)
+
+    pair(3 * rows, rows, 0, group)
+    row_t, cost_t = row_rad[...].T, row_cost[...].T
+    for k in range(4):
+        at = pl.ds(pl.multiple_of(image_order[k] * rows, rows), rows)
+        stat_i[0:8, at] = row_t[0:8, k * rows : (k + 1) * rows]
+        stat_i[8:16, at] = cost_t[0:8, k * rows : (k + 1) * rows]
+        at = pl.ds(pl.multiple_of(text_order[k] * rows, rows), rows)
+        stat_t[0:8, at] = col_rad[0:8, k * rows : (k + 1) * rows]
 
     def width_at(k):
         return pl.ds(pl.multiple_of(k * width, 128), width)
 
     def txt_part(k):
-        gt_snd[k] = (
-            scale * jnp.dot(slope_t[...], zi[:, width_at(k)], preferred_element_type=F32)
-        ).astype(BF16)
+        part = (scale * jnp.dot(slope_t[...], zi[:, width_at(k)], preferred_element_type=F32)).astype(BF16)
+        for r in range(4):
+            at = pl.ds(pl.multiple_of(text_order[r] * rows, rows), rows)
+            gt_snd[k, at] = part[r * rows : (r + 1) * rows]
 
     def img_part(k):
-        gi_snd[k] = (
-            scale * jnp.dot(slope[...], zt[:, width_at(k)], preferred_element_type=F32)
-        ).astype(BF16)
+        part = (scale * jnp.dot(slope[...], zt[:, width_at(k)], preferred_element_type=F32)).astype(BF16)
+        for r in range(4):
+            at = pl.ds(pl.multiple_of(image_order[r] * rows, rows), rows)
+            gi_snd[k, at] = part[r * rows : (r + 1) * rows]
 
     class RingSum:
         def __init__(self, snd, mrg, rcv):
@@ -281,14 +297,22 @@
     row_rad[...] = jnp.broadcast_to(stat_tot[0:1, :], (rows, group)).T
     cost_out[...] = stat_tot[8:9, pl.ds(pl.multiple_of(q * rows, rows), rows)] * (1.0 / total_rows)
 
-    def change(out, unit, inverse, k, column, total):
+    def change(out, unit, inverse, k, role, column, total):
         at = pl.ds(k * rows, rows)
-        u = unit[at, width_at(column)].astype(F32)
-        out[at, :] = ((total - u * row_rad[at, 0:1]) * inverse[at, 0:1]).astype(BF16)
+        placed = pl.ds(pl.multiple_of(role * rows, rows), rows)
+        u = unit[placed, width_at(column)].astype(F32)
+        out[at, :] = ((total - u * row_rad[at, 0:1]) * inverse[placed, 0:1]).astype(BF16)
+
+    def image_role(k):
+        return 2 * lax.rem(k // 2 + y, 2) + lax.rem(k % 2 + c, 2)
+
+    def text_role(k):
+        ahead = lax.rem(k - x + 4, 4)
+        return ahead + lax.div(ahead, 2) * (5 - 2 * ahead)
 
     img_sum.arrive()
     for k in range(4):
-        change(d_img, zi, inv_i, k, q, img_sum.total(k * rows, rows))
+        change(d_img, zi, inv_i, k, image_role(k), q, img_sum.total(k * rows, rows))
 
     own_i, own_t = 16 * f_i.shape[1], 16 * f_t.shape[1]
     cut_i, cut_t = own_i - 48, own_t - 64
@@ -319,9 +343,9 @@
     row_rad[...] = jnp.broadcast_to(txt_total, (rows, group)).T
     txt_sum.arrive()
     for k in range(2):
-        change(d_txt, zt, inv_t, k, x, txt_sum.top(k * rows, rows))
+        change(d_txt, zt, inv_t, k, text_role(k), x, txt_sum.top(k * rows, rows))
     for k in range(2):
-        change(d_txt, zt, inv_t, 2 + k, x, txt_sum.low(k * rows, rows))
+        change(d_txt, zt, inv_t, 2 + k, text_role(2 + k), x, txt_sum.low(k * rows, rows))
 
     part_t = PairSum(et_snd, et_mrg, et_rcv)
     for k in range(4):
@@ -340,7 +364,6 @@
     part_t.merge()
     part_1.merge()
 
-    plus, minus = ring_z // 2, (ring_z - 1) // 2
     own_sem = [slot() for _ in range(12)]
 
     def units(value):
@@ -373,46 +396,58 @@
 
     kept = []
 
+    def one_of(k, unit):
+        return pl.ds(2 * lax.rem(k + ring_z, ring_z) + unit, 1)
+
     def chain(p):
-        p_sem = [slot() for _ in range(plus)]
-        m_sem = [slot() for _ in range(minus)]
-        for s in range(plus):
-            value = tile[p, at_z(z + plus - s)]
-            if s:
-                recv(z_rcv.at[p, s - 1], p_sem[s - 1])
-                value = value + z_rcv[p, s - 1].astype(F32)
-            z_snd[p, s] = value.astype(BF16)
-            send(z_snd.at[p, s], z_rcv.at[p, s], p_sem[s], ZR)
-            if s < minus:
-                value = tile[p, at_z(z - (minus - s))]
-                if s:
-                    recv(z_rcv.at[p, plus + s - 1], m_sem[s - 1])
-                    value = value + z_rcv[p, plus + s - 1].astype(F32)
-                z_snd[p, plus + s] = value.astype(BF16)
-                send(z_snd.at[p, plus + s], z_rcv.at[p, plus + s], m_sem[s], ZL)
-            yield
-        recv(z_rcv.at[p, plus + minus - 1], m_sem[minus - 1])
-        recv(z_rcv.at[p, plus - 1], p_sem[plus - 1])
-        value = tile[p, at_z(z)] + z_rcv[p, plus - 1].astype(F32) + z_rcv[p, plus + minus - 1].astype(F32)
-        y_snd[p] = value.astype(BF16)
+        out, got = z_snd.at[p], z_rcv.at[p]
+        sems = [slot() for _ in range(8)]
+        for i, k in enumerate((4, 3, -3, 1, -1)):
+            out[i] = tile[p, at_z(z + k)].astype(BF16)
+        send(out.at[0, pl.ds(0, 1)], got.at[0, pl.ds(0, 1)], sems[0], Z[2])
+        send(out.at[0, pl.ds(1, 1)], got.at[0, pl.ds(1, 1)], sems[1], Z[-2])
+        send(out.at[1], got.at[1], sems[2], Z[1])
+        send(out.at[2], got.at[2], sems[3], Z[-1])
+        send(out.at[3], got.at[3], sems[4], Z[1])
+        send(out.at[4], got.at[4], sems[5], Z[-1])
+        yield
+        recv(got.at[1], sems[2])
+        recv(got.at[0, pl.ds(0, 1)], sems[0])
+        out[5] = (tile[p, at_z(z + 2)] + got[1].astype(F32)).astype(BF16)
+        out[5, 0:1] = (tile[p, one_of(z + 2, 0)] + got[1, 0:1].astype(F32) + got[0, 0:1].astype(F32)).astype(BF16)
+        send(out.at[5], got.at[5], sems[6], Z[2])
+        recv(got.at[2], sems[3])
+        recv(got.at[0, pl.ds(1, 1)], sems[1])
+        out[6] = (tile[p, at_z(z - 2)] + got[2].astype(F32)).astype(BF16)
+        out[6, 1:2] = (tile[p, one_of(z - 2, 1)] + got[2, 1:2].astype(F32) + got[0, 1:2].astype(F32)).astype(BF16)
+        send(out.at[6], got.at[6], sems[7], Z[-2])
+        yield
+        for i in (3, 4):
+            recv(got.at[i], sems[i + 1])
+        value = tile[p, at_z(z)] + got[3].astype(F32) + got[4].astype(F32)
+        for i in (5, 6):
+            recv(got.at[i], sems[i + 1])
+        y_snd[p] = (value + got[5].astype(F32) + got[6].astype(F32)).astype(BF16)
         y_sem = slot()
         send(y_snd.at[p], y_rcv.at[p], y_sem, YH)
         yield
         recv(y_rcv.at[p], y_sem)
         res[p, at_z(z)] = (y_snd[p].astype(F32) + y_rcv[p].astype(F32)).astype(BF16)
-        p_sem = [slot() for _ in range(plus)]
-        m_sem = [slot() for _ in range(minus)]
-        for s in range(plus):
-            if s:
-                recv(res.at[p, at_z(z - s)], p_sem[s - 1])
-            send(res.at[p, at_z(z - s)], res.at[p, at_z(z - s)], p_sem[s], ZR)
-            if s < minus:
-                if s:
-                    recv(res.at[p, at_z(z + s)], m_sem[s - 1])
-                send(res.at[p, at_z(z + s)], res.at[p, at_z(z + s)], m_sem[s], ZL)
-            yield
-        recv(res.at[p, at_z(z + minus)], m_sem[minus - 1])
-        recv(res.at[p, at_z(z - plus)], p_sem[plus - 1])
+        sems = [slot() for _ in range(8)]
+        mine = res.at[p, at_z(z)]
+        for i, k in enumerate((2, -2, 1, -1)):
+            send(mine, mine, sems[i], Z[k])
+        yield
+        for i, side, unit in ((0, 2, 0), (1, -2, 1)):
+            near, part = res.at[p, at_z(z - side)], res.at[p, one_of(z - side, unit)]
+            recv(near, sems[i])
+            send(part, part, sems[4 + i], Z[side])
+            send(near, near, sems[6 + i], Z[side // 2])
+        yield
+        for i, side, unit in ((0, 2, 0), (1, -2, 1)):
+            recv(res.at[p, at_z(z - side // 2)], sems[2 + i])
+            recv(res.at[p, one_of(z - 2 * side, unit)], sems[4 + i])
+            recv(res.at[p, at_z(z - side - side // 2)], sems[6 + i])
         to_owners(p)
         yield
 
@@ -486,7 +521,7 @@
                 pltpu.SMEM((1,), F32), pltpu.SMEM((1,), F32),
                 B(deep_i, embed), B(deep_t, embed), B(4, rows, deep_i), B(4, rows, deep_t),
                 B(group, embed), B(group, embed), F(group, rows), F(group, rows), F(rows, embed),
-                F(group, rows), F(group, rows), F(group, rows), F(16, group),
+                F(group, rows), F(group, rows), F(group, rows), F(group, rows), F(8, group), F(16, group),
                 B(group, group), B(group, group), F(16, group), F(8, group),
                 F(3, 16, group), F(3, 8, group), F(16, group),
                 B(4, group, width), B(2, group // 2, width), B(6, group // 2, width),

time: 97.9 us -> 86.8 us (0.89)
  Pallas kernels: 95.8 us -> 84.8 us
    pallas_call x1, Pallas kernels: 93.7 us -> 82.7 us  [on_device(): pl.pallas_call(functools.partial(kernel, blocks * rows, ring_z), out_shap...]
where the time goes in v3:
time: 86.8 us; the launch traced here: 86.7 us
  Pallas kernels  84.8 us (98%)
  between operations  1.93 us (2%)
    pallas_call x1, Pallas kernels, on_device(): pl.pallas_call(functools.partial(kernel, blocks * rows, ring_z), out_shap...  82.7 us
    pallas_call x1, Pallas kernels, on_device(): pl.pallas_call(widen, out_shape=(jax.ShapeDtypeStruct((1, rows), F32), ja...  2.11 us

profile of v3, /device:TPU:1, one launch (start us, length us, event | category | flops | bytes accessed | tf_op | source)
XLA Modules:
  0.0 86.7 jit_solution(15867384187413660978)
XLA Ops:
  1.9 82.7 %contrastive_step.1 = (f32[1,128]{1,0:T(1,128)}, bf16[4,7,16,384]{3,2,1,0:T(8,128)(2,1)}, bf16[4,5,16,384]{3,2,1,0:T(8,128)(2,1)}) custom-call(s32[16,128]{1,0:T(8,128)} %bitcast.2, s32[1,16]{1,0:T(1,128)} %tal_hbm.1, f32[1]{0:T(128)S(6)} %copy.11.sha_hbm, f32[1]{0:T(128)S(6)} %copy.12.shi_hbm, bf16[128,1792]{1,0:T(8,128)(2,1)} %x_hbm.1, ...), custom_call_target="tpu_custom_call" | custom-call | tf_op jit(solution)/shard_map/contrastive_step/pallas_call | solution.py:510
  84.6 2.1 %widen.1 = (f32[1,128]{1,0:T(1,128)}, f32[112,1536]{1,0:T(8,128)}, f32[80,1536]{1,0:T(8,128)}) custom-call(f32[1,128]{1,0:T(1,128)} %get-tuple-element.9.cost, bf16[4,7,16,384]{3,2,1,0:T(8,128)(2,1)} %get-tuple-element.10.images, bf16[4,5,16,384]{3,2,1,0:T(8,128)(2,1)} %get-tuple-element.11.texts), custom_call_target="tpu_custom_call" | custom-call | tf_op jit(solution)/shard_map/widen/pallas_call | solution.py:547

commit v4 on v3

--- a/solution.py
+++ b/solution.py
@@ -108,18 +108,22 @@
         wide = jnp.broadcast_to(labels[pl.ds(block, 1), :].astype(F32), (rows, rows))
         lab_i[pl.ds(k * rows, rows), :] = wide.T
 
-    def project(source, weights, unit, inverse, k, role):
+    def project(source, weights, unit, inverse, slots, role):
+        n_rows = rows * len(slots)
+        place = pl.ds(0, n_rows)
+
         def body(j, carry):
             cols = pl.ds(pl.multiple_of(j * 512, 512), 512)
-            u_scr[:, cols] = jnp.dot(source[k], weights[:, cols], preferred_element_type=F32)
+            left = source[slots[0]] if len(slots) == 1 else jnp.concatenate([source[k] for k in slots], axis=0)
+            u_scr[place, cols] = jnp.dot(left, weights[:, cols], preferred_element_type=F32)
             return carry
 
         lax.fori_loop(0, embed // 512, body, 0)
-        u = u_scr[...]
+        u = u_scr[place, :]
         inv = 1.0 / jnp.sqrt(jnp.sum(u * u, axis=1, keepdims=True) + epsilon)
-        at = pl.ds(role * rows, rows)
+        at = pl.ds(role * rows, n_rows)
         unit[at, :] = (u * inv).astype(BF16)
-        inverse[at, :] = jnp.broadcast_to(inv, (rows, rows))
+        inverse[at, :] = jnp.broadcast_to(inv, (n_rows, rows))
 
     scale = sharp[0]
     bias = shift[0]
@@ -153,43 +157,51 @@
     for k in range(4):
         row_alive[k * rows : (k + 1) * rows, :] = jnp.where(down < tally[0, 4 * x + image_order[k]], 1.0, 0.0)
 
+    unit_sem = [slot() for _ in range(4)]
+
+    def role_rows(role):
+        return pl.ds(role * rows, rows)
+
+    def share(role, sem):
+        send(zi.at[role_rows(role)], zi.at[role_rows(role + 1)], unit_sem[sem], PT)
+        send(inv_i.at[role_rows(role)], inv_i.at[role_rows(role + 1)], unit_sem[sem + 1], PT)
+
+    def shared(role, sem):
+        recv(zi.at[role_rows(role + 1)], unit_sem[sem])
+        recv(inv_i.at[role_rows(role + 1)], unit_sem[sem + 1])
+
     loc[2].wait()
-    project(tg, wt, zt, inv_t, x, 0)
+    project(tg, wt, zt, inv_t, (x,), 0)
     recv(tg.at[xl, halves[0]], t_sem[0])
     send(tg.at[xl, halves[0]], tg.at[xl, halves[0]], t_sem[4], XR)
     recv(tg.at[xr, halves[1]], t_sem[1])
     send(tg.at[xr, halves[1]], tg.at[xr, halves[1]], t_sem[5], XL)
     loc[3].wait()
-    project(xg, wv, zi, inv_i, q, 0)
-    recv(xg.at[qp], x_sem[2])
+    project(xg, wv, zi, inv_i, (q,), 0)
+    share(0, 0)
     recv(xg.at[qn, halves[0]], x_sem[0])
     send(xg.at[qn, halves[0]], xg.at[qn, halves[0]], x_sem[3], PT)
-    project(xg, wv, zi, inv_i, qp, 1)
+    shared(0, 0)
+    for k in range(2):
+        pair(k * rows, rows, 0, rows)
     recv(tg.at[xr, halves[0]], t_sem[3])
-    project(tg, wt, zt, inv_t, xr, 1)
+    recv(tg.at[xl, halves[1]], t_sem[2])
+    project(tg, wt, zt, inv_t, (xr, xl), 1)
+    for k in range(2):
+        pair(k * rows, rows, rows, 2 * rows)
     recv(xg.at[qn, halves[1]], x_sem[1])
     send(xg.at[qn, halves[1]], xg.at[qn, halves[1]], x_sem[4], PT)
-    recv(tg.at[xl, halves[1]], t_sem[2])
-    project(tg, wt, zt, inv_t, xl, 2)
-    project(xg, wv, zi, inv_i, qn, 2)
-    for k in range(3):
-        pair(k * rows, rows, 0, 3 * rows)
+    project(xg, wv, zi, inv_i, (qn,), 2)
+    share(2, 2)
     recv(tg.at[xo, halves[0]], t_sem[4])
     recv(tg.at[xo, halves[1]], t_sem[5])
-    project(tg, wt, zt, inv_t, xo, 3)
-    pair(0, 3 * rows, 3 * rows, rows)
-    recv(xg.at[qd, halves[0]], x_sem[3])
-    recv(xg.at[qd, halves[1]], x_sem[4])
-    project(xg, wv, zi, inv_i, qd, 3)
+    project(tg, wt, zt, inv_t, (xo,), 3)
+    for k in range(2):
+        pair(k * rows, rows, 3 * rows, rows)
+    pair(2 * rows, rows, 0, group)
+    shared(2, 2)
 
     pair(3 * rows, rows, 0, group)
-    row_t, cost_t = row_rad[...].T, row_cost[...].T
-    for k in range(4):
-        at = pl.ds(pl.multiple_of(image_order[k] * rows, rows), rows)
-        stat_i[0:8, at] = row_t[0:8, k * rows : (k + 1) * rows]
-        stat_i[8:16, at] = cost_t[0:8, k * rows : (k + 1) * rows]
-        at = pl.ds(pl.multiple_of(text_order[k] * rows, rows), rows)
-        stat_t[0:8, at] = col_rad[0:8, k * rows : (k + 1) * rows]
 
     def width_at(k):
         return pl.ds(pl.multiple_of(k * width, 128), width)
@@ -266,18 +278,24 @@
             at = pl.ds(start, size)
             return self.snd[q, at].astype(F32) + self.rcv[1, at].astype(F32) + self.rcv[2, at].astype(F32)
 
-    st_sem = [slot() for _ in range(6)]
-    for i, dev in enumerate((XR, XL, XO)):
-        send(stat_t, stt_rcv.at[i], st_sem[i], dev)
-    for i, dev in enumerate((PT, YN, DG)):
-        send(stat_i, sti_rcv.at[i], st_sem[3 + i], dev)
-
     txt_sum = RingSum(gt_snd, gt_mrg, gt_rcv)
     img_sum = PairSum(gi_snd, gi_mrg, gi_rcv)
     txt_part(xo)
     txt_sum.far()
     img_part(qd)
     img_sum.far()
+    row_t, cost_t = row_rad[...].T, row_cost[...].T
+    for k in range(4):
+        at = pl.ds(pl.multiple_of(image_order[k] * rows, rows), rows)
+        stat_i[0:8, at] = row_t[0:8, k * rows : (k + 1) * rows]
+        stat_i[8:16, at] = cost_t[0:8, k * rows : (k + 1) * rows]
+        at = pl.ds(pl.multiple_of(text_order[k] * rows, rows), rows)
+        stat_t[0:8, at] = col_rad[0:8, k * rows : (k + 1) * rows]
+    st_sem = [slot() for _ in range(6)]
+    for i, dev in enumerate((XR, XL, XO)):
+        send(stat_t, stt_rcv.at[i], st_sem[i], dev)
+    for i, dev in enumerate((PT, YN, DG)):
+        send(stat_i, sti_rcv.at[i], st_sem[3 + i], dev)
     txt_part(xr)
     txt_part(xl)
     txt_sum.near()
@@ -288,6 +306,9 @@
     img_part(q)
     txt_part(x)
     txt_sum.merge()
+    recv(xg.at[qp], x_sem[2])
+    recv(xg.at[qd, halves[0]], x_sem[3])
+    recv(xg.at[qd, halves[1]], x_sem[4])
     for k in range(4):
         xg_t[:, k * rows : (k + 1) * rows] = xg[k].T
 
@@ -520,7 +541,7 @@
                 pltpu.VMEM((blocks, rows), jnp.int32), pltpu.SMEM((1, blocks), jnp.int32),
                 pltpu.SMEM((1,), F32), pltpu.SMEM((1,), F32),
                 B(deep_i, embed), B(deep_t, embed), B(4, rows, deep_i), B(4, rows, deep_t),
-                B(group, embed), B(group, embed), F(group, rows), F(group, rows), F(rows, embed),
+                B(group, embed), B(group, embed), F(group, rows), F(group, rows), F(2 * rows, embed),
                 F(group, rows), F(group, rows), F(group, rows), F(group, rows), F(8, group), F(16, group),
                 B(group, group), B(group, group), F(16, group), F(8, group),
                 F(3, 16, group), F(3, 8, group), F(16, group),

time: 86.8 us -> 85.4 us (0.984)
  Pallas kernels: 84.8 us -> 83.4 us
    pallas_call x1, Pallas kernels: 82.7 us -> 81.2 us  [on_device(): pl.pallas_call(functools.partial(kernel, blocks * rows, ring_z), out_shap...]
where the time goes in v4:
time: 85.4 us; the launch traced here: 85.3 us
  Pallas kernels  83.4 us (98%)
  between operations  1.93 us (2%)
    pallas_call x1, Pallas kernels, on_device(): pl.pallas_call(functools.partial(kernel, blocks * rows, ring_z), out_shap...  81.2 us
    pallas_call x1, Pallas kernels, on_device(): pl.pallas_call(widen, out_shape=(jax.ShapeDtypeStruct((1, rows), F32), ja...  2.11 us

profile of v4, /device:TPU:1, one launch (start us, length us, event | category | flops | bytes accessed | tf_op | source)
XLA Modules:
  0.0 85.3 jit_solution(17012871320478081146)
XLA Ops:
  1.9 81.2 %contrastive_step.1 = (f32[1,128]{1,0:T(1,128)}, bf16[4,7,16,384]{3,2,1,0:T(8,128)(2,1)}, bf16[4,5,16,384]{3,2,1,0:T(8,128)(2,1)}) custom-call(s32[16,128]{1,0:T(8,128)} %bitcast.2, s32[1,16]{1,0:T(1,128)} %tal_hbm.1, f32[1]{0:T(128)S(6)} %copy.11.sha_hbm, f32[1]{0:T(128)S(6)} %copy.12.shi_hbm, bf16[128,1792]{1,0:T(8,128)(2,1)} %x_hbm.1, ...), custom_call_target="tpu_custom_call" | custom-call | tf_op jit(solution)/shard_map/contrastive_step/pallas_call | solution.py:531
  83.2 2.1 %widen.1 = (f32[1,128]{1,0:T(1,128)}, f32[112,1536]{1,0:T(8,128)}, f32[80,1536]{1,0:T(8,128)}) custom-call(f32[1,128]{1,0:T(1,128)} %get-tuple-element.9.cost, bf16[4,7,16,384]{3,2,1,0:T(8,128)(2,1)} %get-tuple-element.10.images, bf16[4,5,16,384]{3,2,1,0:T(8,128)(2,1)} %get-tuple-element.11.texts), custom_call_target="tpu_custom_call" | custom-call | tf_op jit(solution)/shard_map/widen/pallas_call | solution.py:568

commit v5 on v4

--- a/solution.py
+++ b/solution.py
@@ -12,13 +12,13 @@
 MESH = pl.DeviceIdType.MESH
 F32 = jnp.float32
 BF16 = jnp.bfloat16
-ORDER = (0, "t", 2, "i", 1) + (0, 2, 1) * 5
+ORDER = (0, "t", 2, "i", 1) + (0, 1, 2) * 5
 
 
 def kernel(
     total_rows, ring_z, lab_hbm, tal_hbm, sha_hbm, shi_hbm, x_hbm, t_hbm, wv_hbm, wt_hbm,
     cost_out, f_i, f_t,
-    labels, tally, sharp, shift,
+    labels, tally, sharp, shift, cost_own,
     wv, wt, xg, tg, zi, zt, inv_i, inv_t, u_scr, lab_i, row_alive, row_rad, row_cost, col_rad, txt_meta,
     slope, slope_t, stat_i, stat_t, sti_rcv, stt_rcv, stat_tot,
     gt_snd, gt_mrg, gt_rcv, gi_snd, gi_mrg, gi_rcv, d_img, d_txt, xg_t, tg_t,
@@ -316,7 +316,9 @@
         recv(sti_rcv.at[i], st_sem[3 + i])
     stat_tot[...] = stat_i[...] + sti_rcv[0] + sti_rcv[1] + sti_rcv[2]
     row_rad[...] = jnp.broadcast_to(stat_tot[0:1, :], (rows, group)).T
-    cost_out[...] = stat_tot[8:9, pl.ds(pl.multiple_of(q * rows, rows), rows)] * (1.0 / total_rows)
+    cost_own[...] = stat_tot[8:9, pl.ds(pl.multiple_of(q * rows, rows), rows)] * (1.0 / total_rows)
+    cost_copy = pltpu.make_async_copy(cost_own, cost_out, loc_sem.at[12])
+    cost_copy.start()
 
     def change(out, unit, inverse, k, role, column, total):
         at = pl.ds(k * rows, rows)
@@ -497,6 +499,7 @@
         recv(f_t.at[k, pl.ds(1, 4)], own_sem[9 + i])
     for copy in kept:
         copy.wait()
+    cost_copy.wait()
 
     for copy in started:
         copy.wait_send()
@@ -536,10 +539,10 @@
                 jax.ShapeDtypeStruct((4, own_t // 16, 16, width), BF16),
             ),
             in_specs=[hbm] * 8,
-            out_specs=(vmem, hbm, hbm),
+            out_specs=(hbm, hbm, hbm),
             scratch_shapes=[
                 pltpu.VMEM((blocks, rows), jnp.int32), pltpu.SMEM((1, blocks), jnp.int32),
-                pltpu.SMEM((1,), F32), pltpu.SMEM((1,), F32),
+                pltpu.SMEM((1,), F32), pltpu.SMEM((1,), F32), F(1, rows),
                 B(deep_i, embed), B(deep_t, embed), B(4, rows, deep_i), B(4, rows, deep_t),
                 B(group, embed), B(group, embed), F(group, rows), F(group, rows), F(2 * rows, embed),
                 F(group, rows), F(group, rows), F(group, rows), F(group, rows), F(8, group), F(16, group),
@@ -553,7 +556,7 @@
                 B(4, nt, width), B(nt, width), B(3, nt, width),
                 F(3, 16, 16, width), B(3, ring_z - 1, 2, 16, width), B(3, ring_z - 1, 2, 16, width),
                 B(3, 2, 16, width), B(3, 2, 16, width), B(3, 16, 16, width),
-                pltpu.SemaphoreType.DMA((12,)),
+                pltpu.SemaphoreType.DMA((13,)),
                 pltpu.SemaphoreType.DMA((128,)),
                 pltpu.SemaphoreType.DMA((128,)),
             ],

time: 85.4 us -> 84.5 us (0.989)
  Pallas kernels: 83.4 us -> 81.6 us
    pallas_call x1, Pallas kernels: 81.2 us -> 79.5 us  [on_device(): pl.pallas_call(functools.partial(kernel, blocks * rows, ring_z), out_shap...]
where the time goes in v5:
time: 84.5 us; the launch traced here: 83.6 us
  Pallas kernels  81.6 us (97%)
  between operations  1.93 us (2%)
    pallas_call x1, Pallas kernels, on_device(): pl.pallas_call(functools.partial(kernel, blocks * rows, ring_z), out_shap...  79.5 us
    pallas_call x1, Pallas kernels, on_device(): pl.pallas_call(widen, out_shape=(jax.ShapeDtypeStruct((1, rows), F32), ja...  2.11 us

profile of v5, /device:TPU:1, one launch (start us, length us, event | category | flops | bytes accessed | tf_op | source)
XLA Modules:
  0.0 83.6 jit_solution(14685029749023761350)
XLA Ops:
  1.9 79.5 %contrastive_step.1 = (f32[1,128]{1,0:T(1,128)}, bf16[4,7,16,384]{3,2,1,0:T(8,128)(2,1)}, bf16[4,5,16,384]{3,2,1,0:T(8,128)(2,1)}) custom-call(s32[16,128]{1,0:T(8,128)} %bitcast.2, s32[1,16]{1,0:T(1,128)} %tal_hbm.1, f32[1]{0:T(128)S(6)} %copy.11.sha_hbm, f32[1]{0:T(128)S(6)} %copy.12.shi_hbm, bf16[128,1792]{1,0:T(8,128)(2,1)} %x_hbm.1, ...), custom_call_target="tpu_custom_call" | custom-call | tf_op jit(solution)/shard_map/contrastive_step/pallas_call | solution.py:534
  81.5 2.1 %widen.1 = (f32[1,128]{1,0:T(1,128)}, f32[112,1536]{1,0:T(8,128)}, f32[80,1536]{1,0:T(8,128)}) custom-call(f32[1,128]{1,0:T(1,128)} %get-tuple-element.9.cost, bf16[4,7,16,384]{3,2,1,0:T(8,128)(2,1)} %get-tuple-element.10.images, bf16[4,5,16,384]{3,2,1,0:T(8,128)(2,1)} %get-tuple-element.11.texts), custom_call_target="tpu_custom_call" | custom-call | tf_op jit(solution)/shard_map/widen/pallas_call | solution.py:571

commit v6 on v5

--- a/solution.py
+++ b/solution.py
@@ -508,10 +508,8 @@
 def widen(cost, images, texts, cost_out, image_out, text_out):
     width = images.shape[-1]
     cost_out[...] = cost[...]
-    for k in range(4):
-        cols = pl.ds(k * width, width)
-        image_out[:, cols] = images[k].reshape(-1, width).astype(F32)
-        text_out[:, cols] = texts[k].reshape(-1, width).astype(F32)
+    image_out[...] = images[0].reshape(-1, width).astype(F32)
+    text_out[...] = texts[0].reshape(-1, width).astype(F32)
 
 
 def solution(mesh):
@@ -526,7 +524,6 @@
         deep_t, embed = caption_mapping_matrix.shape
         group, width = 4 * rows, embed // 4
         own_i, own_t = deep_i // blocks, deep_t // blocks
-        vmem = pl.BlockSpec(memory_space=pltpu.VMEM)
         hbm = pl.BlockSpec(memory_space=pl.ANY)
         B = lambda *shape: pltpu.VMEM(shape, BF16)
         F = lambda *shape: pltpu.VMEM(shape, F32)
@@ -575,8 +572,17 @@
                 jax.ShapeDtypeStruct((own_i, embed), F32),
                 jax.ShapeDtypeStruct((own_t, embed), F32),
             ),
-            in_specs=[vmem] * 3,
-            out_specs=(vmem,) * 3,
+            grid=(4,),
+            in_specs=[
+                pl.BlockSpec((1, rows), lambda k: (0, 0)),
+                pl.BlockSpec((1, own_i // 16, 16, width), lambda k: (k, 0, 0, 0)),
+                pl.BlockSpec((1, own_t // 16, 16, width), lambda k: (k, 0, 0, 0)),
+            ],
+            out_specs=(
+                pl.BlockSpec((1, rows), lambda k: (0, 0)),
+                pl.BlockSpec((own_i, width), lambda k: (0, k)),
+                pl.BlockSpec((own_t, width), lambda k: (0, k)),
+            ),
             name="widen",
         )(cost, images, texts)
         return cost.reshape(rows), grad_image, grad_text

time: 84.5 us -> 85.8 us (1.015)
  Pallas kernels: 81.6 us -> 82.8 us
    pallas_call x1, Pallas kernels: 2.11 us -> 3.25 us  [on_device(): pl.pallas_call(widen, out_shape=(jax.ShapeDtypeStruct((1, rows), F32), ja...]
where the time goes in v6:
time: 85.8 us; the launch traced here: 84.7 us
  Pallas kernels  82.8 us (97%)
  between operations  1.93 us (2%)
    pallas_call x1, Pallas kernels, on_device(): pl.pallas_call(functools.partial(kernel, blocks * rows, ring_z), out_shap...  79.5 us
    pallas_call x1, Pallas kernels, on_device(): pl.pallas_call(widen, out_shape=(jax.ShapeDtypeStruct((1, rows), F32), ja...  3.25 us

profile of v6, /device:TPU:1, one launch (start us, length us, event | category | flops | bytes accessed | tf_op | source)
XLA Modules:
  0.0 84.7 jit_solution(17282683591518831300)
XLA Ops:
  1.9 79.5 %contrastive_step.1 = (f32[1,128]{1,0:T(1,128)}, bf16[4,7,16,384]{3,2,1,0:T(8,128)(2,1)}, bf16[4,5,16,384]{3,2,1,0:T(8,128)(2,1)}) custom-call(s32[16,128]{1,0:T(8,128)} %bitcast.2, s32[1,16]{1,0:T(1,128)} %tal_hbm.1, f32[1]{0:T(128)S(6)} %copy.11.sha_hbm, f32[1]{0:T(128)S(6)} %copy.12.shi_hbm, bf16[128,1792]{1,0:T(8,128)(2,1)} %x_hbm.1, ...), custom_call_target="tpu_custom_call" | custom-call | tf_op jit(solution)/shard_map/contrastive_step/pallas_call | solution.py:531
  81.5 3.3 %widen.1 = (f32[1,128]{1,0:T(1,128)}, f32[112,1536]{1,0:T(8,128)}, f32[80,1536]{1,0:T(8,128)}) custom-call(f32[1,128]{1,0:T(1,128)} %get-tuple-element.9.cost, bf16[4,7,16,384]{3,2,1,0:T(8,128)(2,1)} %get-tuple-element.10.images, bf16[4,5,16,384]{3,2,1,0:T(8,128)(2,1)} %get-tuple-element.11.texts), custom_call_target="tpu_custom_call" | custom-call | tf_op jit(solution)/shard_map/widen/pallas_call | solution.py:568
